TPU v7x, 128 devices: a whole 4x4x4 slice. The times are simulated.
128 devices in a mesh: seq: 16 (over z, y), tensor: 8 (over x, core).
Axes of the slice: x: 4, y: 4, z: 4, core: 2. Of those that a mesh axis runs over, the one named last changes fastest.
Arguments:
- tokens: bfloat16 [256, 4, 3072], P('seq'), may hold values from -6 to 6
- lengths: int32 [256], replicated, may hold values from 1 to 16384, as said below
- page_request: int32 [2048], P('seq'), may hold values from 0 to 255, as said below
- page_block: int32 [2048], P('seq'), may hold values from 0 to 128, as said below
- k_cache: bfloat16 [2048, 8, 128, 128], P('seq', 'tensor'), may hold values from -330 to 330
- v_cache: bfloat16 [2048, 8, 128, 128], P('seq', 'tensor'), may hold values from -6 to 6
- attn_gain: bfloat16 [3072], replicated, may hold values from 0.099609375 to 1.8984375
- w_query: bfloat16 [3072, 3072], P(None, 'tensor'), may hold values from -0.109375 to 0.109375
- w_key: bfloat16 [3072, 1024], P(None, 'tensor'), may hold values from -0.109375 to 0.109375
- w_value: bfloat16 [3072, 1024], P(None, 'tensor'), may hold values from -0.109375 to 0.109375
- w_out: bfloat16 [3072, 3072], P('tensor'), may hold values from -0.109375 to 0.109375
- mlp_gain: bfloat16 [3072], replicated, may hold values from 0.099609375 to 1.8984375
- w_gate: bfloat16 [3072, 4096], P(None, 'tensor'), may hold values from -0.109375 to 0.109375
- w_up: bfloat16 [3072, 4096], P(None, 'tensor'), may hold values from -0.109375 to 0.109375
- w_down: bfloat16 [4096, 3072], P('tensor'), may hold values from -0.09375 to 0.09375
Outputs:
- layer_out: bfloat16 [256, 4, 3072], P('seq', None, 'tensor')
Inputs may be any that keep to these rules, and one draw needn't show every extreme that they name: `lengths`: A request r whose index is a multiple of 32 has a long cache, within 128 tokens of 16384; the others have at most 511. Request 0 has exactly 16384. `page_request`: each pair of a long request and a page number below 128, or of a short request and a page number below 4, appears in exactly one slot; slots of pages at or beyond a request's length hold no used position. A short request's pages lie in the slots of the seq index that holds its tokens. `page_block`: slots of page number 128 hold no used position.
All inputs are finite; a program needn't handle non-finite values.
Results may differ from a plain program's by a relative error of at most 0.012.
Values may be sent and summed in bfloat16 or wider, within the bound.
No kernel may reach another device: no remote copies, remote signals or barrier semaphores. Data moves between devices by JAX's collectives and lax.ppermute only.
A program may use at most 128 MiB of HBM per device.

v0:
```python
import math

import jax
import jax.numpy as jnp
import numpy as np
from jax import lax
from jax.experimental import pallas as pl
from jax.experimental.pallas import tpu as pltpu
from jax.sharding import PartitionSpec as P


EPSILON = 1e-05
NEGATIVE = -1e30
ROPE_BASE = 500000.0
F32 = jnp.float32
BF16 = jnp.bfloat16

SEQ = 16
TEN = 8
D = 3072
HD = 128
PAGE = 128
REQ_DEV = 16
NEW = 4
G = 3
ROWS = REQ_DEV * NEW
QCOLS = G * HD
COLS = D // TEN
FF_DEV = 512
SLOTS = 128
LONG_STEP = 32
LONGS = 8
SHORT_BLK = 4
SCALE = 1.0 / math.sqrt(HD)
CHUNK = 8


VMEM = pl.BlockSpec(memory_space=pltpu.VMEM)
SMEM = pl.BlockSpec(memory_space=pltpu.SMEM)
HBM = pl.BlockSpec(memory_space=pltpu.HBM)
MIB = 1 << 20


def call(kernel, out_shape, in_specs, scratch, limit, out_specs=None):
    return pl.pallas_call(
        kernel,
        out_shape=out_shape,
        in_specs=in_specs,
        out_specs=out_specs or jax.tree.map(lambda _: VMEM, out_shape),
        scratch_shapes=scratch,
        compiler_params=pltpu.CompilerParams(vmem_limit_bytes=limit * MIB),
    )


def sds(shape, dtype):
    return jax.ShapeDtypeStruct(shape, dtype)


def nt_dot(a, b):
    return lax.dot_general(a, b, (((1,), (1,)), ((), ())), preferred_element_type=F32)


def nn_dot(a, b):
    return jnp.dot(a, b, preferred_element_type=F32)


def iota(shape, dim):
    return lax.broadcasted_iota(jnp.int32, shape, dim)


def start_all(pairs, sems):
    copies = [pltpu.make_async_copy(src, dst, sems.at[i]) for i, (src, dst) in enumerate(pairs)]
    for copy in copies:
        copy.start(priority=1)
    return copies


def qkv_kernel(
    lengths_h, request_h, block_h, tok_h, gain_h, inv_h, wq_h, wk_h, wv_h,
    q_pack, k_new, v_new, q_long, table,
    lengths, request, block, tok, gain, inv, wq, wk, wv, x_s, pos_s, t_s, table_s, sems, table_sem,
):
    third = D // 3
    copies = start_all(
        [(tok_h, tok), (gain_h, gain), (lengths_h, lengths), (inv_h, inv)]
        + [(wq_h.at[pl.ds(i * third, third)], wq.at[pl.ds(i * third, third)]) for i in range(3)]
        + [(wk_h, wk), (wv_h, wv), (request_h, request.at[0]), (block_h, block.at[0])],
        sems,
    )
    home = lax.axis_index("seq") * REQ_DEV
    copies[9].wait()
    copies[10].wait()
    copies[2].wait()
    req = jnp.broadcast_to(request[...], (8, SLOTS))
    blk = jnp.broadcast_to(block[...], (8, SLOTS))
    lane = iota((8, SLOTS), 1)
    long_len = jnp.zeros((8, SLOTS), jnp.int32)
    for k in range(LONGS):
        long_len = jnp.where(req == k * LONG_STEP, lengths[k * LONG_STEP], long_len)
    limit = long_len - blk * PAGE
    key = jnp.where(limit > 0, req // LONG_STEP, LONGS)
    start = jnp.zeros((8, SLOTS), F32)
    first = jnp.zeros((8, SLOTS), F32)
    for k in range(LONGS):
        held = jnp.sum(jnp.where(key == k, 1.0, 0.0), axis=1, keepdims=True)
        first = jnp.where(key == k, start, first)
        start = start + jnp.floor((held + (CHUNK - 1)) * (1.0 / CHUNK)) * CHUNK
    packed = lane + key * 128 + jnp.minimum(limit, PAGE) * 1024
    mine = (req >= home) & (req < home + REQ_DEV) & (blk < SHORT_BLK)
    index = jnp.where(mine, (req - home) * SHORT_BLK + blk, -1)
    slot = iota((SLOTS, SLOTS), 0)
    spot = iota((SLOTS, SLOTS), 1)

    def column(row):
        wide = jnp.broadcast_to(row[0:1, :].astype(F32), (SLOTS, SLOTS))
        return jnp.sum(jnp.where(slot == spot, wide, 0.0), axis=1, keepdims=True)

    def scatter(at, value):
        return jnp.sum(jnp.where(at == spot.astype(F32), value, 0.0), axis=0, keepdims=True).astype(jnp.int32)

    table_s[0:1, :] = scatter(column(index), slot.astype(F32))
    keys = key[0:1, :].astype(F32)
    ahead = jnp.sum(jnp.where((column(key) == keys) & (slot < spot), 1.0, 0.0), axis=0, keepdims=True)
    at = column(jnp.where(keys < LONGS, first[0:1, :] + ahead, -1.0))
    words = column(packed)
    table_s[1:2, :] = scatter(at, words)
    table_s[2:3, :] = scatter(at - SLOTS, words)
    facts = jnp.where(lane == 0, (start * (1.0 / CHUNK)).astype(jnp.int32), 0)
    for r in range(REQ_DEV):
        known = jnp.where((home + r) % LONG_STEP == 0, 0, lengths[home + r])
        facts = jnp.where(lane == 16 + r, known, facts)
    table_s[3:4, :] = facts[0:1, :]
    table_s[4:8, :] = jnp.zeros((4, SLOTS), jnp.int32)
    give = pltpu.make_async_copy(table_s, table, table_sem)
    give.start()
    copies[0].wait()
    for r in range(REQ_DEV):
        x_s[r * NEW : (r + 1) * NEW, :] = tok[r].astype(F32)
    x = x_s[...]
    mean_square = jnp.mean(x * x, axis=-1, keepdims=True)
    copies[1].wait()
    normed = (x * lax.rsqrt(mean_square + EPSILON) * gain[...].astype(F32).reshape(1, D)).astype(BF16)
    for r in range(REQ_DEV):
        pos_s[r * NEW : (r + 1) * NEW, :] = lengths[home + r] + iota((NEW, HD), 0)
    copies[3].wait()
    angle = pos_s[...].astype(F32) * inv[...]
    cosine = jnp.cos(angle)
    sine = jnp.sin(angle)
    sine = jnp.where(iota((ROWS, HD), 1) < HD // 2, -sine, sine)

    def rope(v):
        return v * cosine + pltpu.roll(v, HD // 2, 1) * sine

    q = jnp.zeros((ROWS, QCOLS), F32)
    for i in range(3):
        copies[4 + i].wait()
        q = q + nn_dot(normed[:, i * third : (i + 1) * third], wq[i * third : (i + 1) * third, :])
    for g in range(G):
        roped = rope(q[:, g * HD : (g + 1) * HD])
        for pair in range(REQ_DEV // 2):
            q_pack[pair * 32 + g * 8 : pair * 32 + g * 8 + 8, :] = roped[pair * 8 : pair * 8 + 8, :]
        t_s[g * NEW : (g + 1) * NEW, :] = roped[0:NEW, :]
    t_s[G * NEW : 16, :] = jnp.zeros((16 - G * NEW, HD), F32)
    for pair in range(REQ_DEV // 2):
        q_pack[pair * 32 + 24 : pair * 32 + 32, :] = jnp.zeros((8, HD), F32)
    packed = t_s[...].astype(BF16)
    for i in range(SEQ):
        q_long[i] = packed
    copies[7].wait()
    k_new[...] = rope(nn_dot(normed, wk[...])).astype(BF16)
    copies[8].wait()
    v_new[...] = nn_dot(normed, wv[...]).astype(BF16)
    give.wait()


def to_row(column, eye):
    return jnp.sum(jnp.where(eye, column, 0.0), axis=0, keepdims=True)


def attend_kernel(
    table, q_pack, k_new, v_new, q_all, k_c, v_h,
    att, part0, part,
    v_c, fresh_s, short_s, top_s, acc_s, sum_s, att_s, o_0, m_0, l_0, long_s, m_s, l_s, o_s, sem,
):
    copy = pltpu.make_async_copy(v_h, v_c, sem)
    copy.start(priority=1)
    row = iota((32, ROWS), 0)
    col = iota((32, ROWS), 1)
    lane = iota((32, PAGE), 1)
    half = iota((32, PAGE), 0) % 8 // NEW

    def pair_score(pair, carry):
        q = q_pack[pl.ds(pl.multiple_of(pair * 32, 32), 32), :].astype(BF16)
        fresh = nt_dot(q, k_new[...]) * SCALE
        fresh_ok = (pair * 2 + row % 8 // NEW == col // NEW) & (col % NEW <= row % NEW)
        fresh = jnp.where(fresh_ok, fresh, NEGATIVE)
        fresh_s[pair] = fresh
        pages = [k_c[table[0, pair * CHUNK + i]] for i in range(CHUNK)]
        s = nt_dot(q, jnp.concatenate(pages, axis=0)) * SCALE
        own = jnp.where(half == 0, table[3, 16 + pair * 2], table[3, 17 + pair * 2])
        tops = []
        for i in range(CHUNK):
            inside = (half == i // SHORT_BLK) & (lane < own - i % SHORT_BLK * PAGE)
            part_s = jnp.where(inside, s[:, i * PAGE : (i + 1) * PAGE], NEGATIVE)
            short_s[pair, :, i * PAGE : (i + 1) * PAGE] = part_s
            tops.append(part_s)
        while len(tops) > 1:
            tops = [jnp.maximum(x, y) for x, y in zip(tops[::2], tops[1::2])]
        m = jnp.maximum(jnp.max(tops[0], axis=1, keepdims=True), jnp.max(fresh, axis=1, keepdims=True))
        top_s[pair] = jnp.broadcast_to(m, (32, HD))
        return carry

    lax.fori_loop(0, REQ_DEV // 2, pair_score, 0, unroll=2)

    trips = (table[3, 0] + 1) // 2
    m_s[...] = jnp.full((LONGS, 16, HD), NEGATIVE, F32)
    l_s[...] = jnp.zeros((LONGS, 16, HD), F32)
    o_s[...] = jnp.zeros((LONGS, 16, HD), F32)
    key_lane = iota((16, PAGE), 1)

    def entries(chunk):
        words = [table[1 + chunk // (SLOTS // CHUNK), chunk % (SLOTS // CHUNK) * CHUNK + i] for i in range(CHUNK)]
        return words, (words[0] >> 7) & 7

    def long_score(j, carry):
        got = []
        for chunk in (2 * j, 2 * j + 1):
            words, key = entries(chunk)
            pages = [k_c[word & 127] for word in words]
            s = nt_dot(q_all[2 * key], jnp.concatenate(pages, axis=0)) * SCALE
            tops = []
            for i, word in enumerate(words):
                part_s = jnp.where(key_lane < (word >> 10), s[:, i * PAGE : (i + 1) * PAGE], NEGATIVE)
                long_s[chunk, :, i * PAGE : (i + 1) * PAGE] = part_s
                tops.append(part_s)
            while len(tops) > 1:
                tops = [jnp.maximum(x, y) for x, y in zip(tops[::2], tops[1::2])]
            got.append((key, tops[0]))
        for key, top in got:
            m_s[key] = jnp.maximum(m_s[key], top)
        return carry

    lax.fori_loop(0, trips, long_score, 0)
    for k in range(LONGS):
        m_s[k] = jnp.broadcast_to(jnp.maximum(jnp.max(m_s[k], axis=1, keepdims=True), 0.1 * NEGATIVE), (16, HD))
    copy.wait()

    def pair_sum(pair, carry):
        m = top_s[pair]
        w = jnp.exp(fresh_s[pair] - m[:, 0:ROWS]).astype(BF16)
        total = jnp.sum(w.astype(F32), axis=1, keepdims=True)
        acc = nn_dot(w, v_new[...])
        ws = [jnp.exp(short_s[pair, :, i * PAGE : (i + 1) * PAGE] - m).astype(BF16) for i in range(CHUNK)]
        pages = [v_c[table[0, pair * CHUNK + i]] for i in range(CHUNK)]
        acc = acc + nn_dot(jnp.concatenate(ws, axis=1), jnp.concatenate(pages, axis=0))
        total = total + jnp.sum(sum(w.astype(F32) for w in ws), axis=1, keepdims=True)
        acc_s[pair] = acc
        sum_s[pair] = jnp.broadcast_to(total, (32, HD))
        out = acc / total
        at = pl.multiple_of(pair * 8, 8)
        for g in range(G):
            att_s[pl.ds(at, 8), g * HD : (g + 1) * HD] = out[g * 8 : (g + 1) * 8, :]
        return carry

    lax.fori_loop(0, REQ_DEV // 2, pair_sum, 0, unroll=2)
    att[...] = att_s[...]
    for g in range(G):
        o_0[g * NEW : (g + 1) * NEW, :] = acc_s[0, g * 8 : g * 8 + NEW, :]
        m_0[g * NEW : (g + 1) * NEW, :] = top_s[0, g * 8 : g * 8 + NEW, :]
        l_0[g * NEW : (g + 1) * NEW, :] = sum_s[0, g * 8 : g * 8 + NEW, :]
    eye = (iota((16, HD), 0) == iota((16, HD), 1)) & (iota((16, HD), 0) < G * NEW)
    part0[...] = o_0[...]
    part0[12:13, :] = to_row(m_0[...], eye)
    part0[13:14, :] = to_row(l_0[...], eye)
    part0[14:16, :] = jnp.zeros((2, HD), F32)

    def long_sum(j, carry):
        got = []
        for chunk in (2 * j, 2 * j + 1):
            words, key = entries(chunk)
            m = m_s[key]
            ws = [jnp.exp(long_s[chunk, :, i * PAGE : (i + 1) * PAGE] - m).astype(BF16) for i in range(CHUNK)]
            pages = [v_c[word & 127] for word in words]
            o = nn_dot(jnp.concatenate(ws, axis=1), jnp.concatenate(pages, axis=0))
            got.append((key, sum(w.astype(F32) for w in ws), o))
        for key, w, o in got:
            l_s[key] = l_s[key] + w
            o_s[key] = o_s[key] + o
        return carry

    lax.fori_loop(0, trips, long_sum, 0)
    for k in range(LONGS):
        total = jnp.broadcast_to(jnp.sum(l_s[k], axis=1, keepdims=True), (16, HD))
        part[2 * k, 0:12, :] = o_s[k, 0:12, :].astype(BF16)
        part[2 * k, 12:14, :] = jnp.concatenate([spread(m_s[k]), spread(total)], axis=0).astype(BF16)
        part[2 * k, 14:16, :] = jnp.zeros((2, HD), BF16)
        part[2 * k + 1] = jnp.zeros((16, HD), BF16)


def spread(column):
    row = iota((16, HD), 0)
    lane = iota((16, HD), 1)
    out = jnp.zeros((16, HD), F32)
    rest = column
    for i in range(3):
        piece = lax.reduce_precision(rest, 8, 7)
        rest = rest - piece
        out = jnp.where((lane == row + 16 * i) & (row < G * NEW), piece, out)
    return jnp.sum(out, axis=0, keepdims=True)


def gathered(row):
    return row + pltpu.roll(row, HD - 16, 1) + pltpu.roll(row, HD - 32, 1)


def place():
    tensor = lax.axis_index("tensor")
    return tensor // 2, tensor % 2


def split_product(a, w, keep, send):
    core = place()[1]
    for x in range(TEN // 2):
        at = pl.multiple_of((2 * x + 1 - core) * COLS, COLS)
        send[x] = nn_dot(a, w[:, pl.ds(at, COLS)]).astype(BF16)
    for x in range(TEN // 2):
        at = pl.multiple_of((2 * x + core) * COLS, COLS)
        keep[x] = nn_dot(a, w[:, pl.ds(at, COLS)]).astype(keep.dtype)


def out_kernel(att, part0, parts, w_out, keep, send, att_s, m_s, l_s):
    att_s[...] = att[...]

    @pl.when(lax.axis_index("seq") % 2 == 0)
    def _():
        for s in range(SEQ):
            stats = parts[s].astype(F32)
            m_s[s : s + 1, :] = stats[12:13, :]
            l_s[s : s + 1, :] = stats[13:14, :]
        m0 = part0[12:13, :]
        m = gathered(m_s[...])
        top = jnp.maximum(jnp.max(m, axis=0, keepdims=True), m0)
        grow = jnp.exp(m - top)
        grow0 = jnp.exp(m0 - top)
        total = jnp.sum(grow * gathered(l_s[...]), axis=0, keepdims=True) + grow0 * part0[13:14, :]
        live = iota((1, HD), 1) < G * NEW
        inverse = jnp.where(live, 1.0 / jnp.where(live, total, 1.0), 0.0)
        eye = iota((16, HD), 0) == iota((16, HD), 1)

        def scaled(o, coef):
            column = jnp.sum(jnp.where(eye, coef, 0.0), axis=1, keepdims=True)
            return o * column

        out = scaled(part0[...], grow0 * inverse)
        coefs = grow * inverse
        for s in range(SEQ):
            out = out + scaled(parts[s].astype(F32), coefs[s : s + 1, :])
        for g in range(G):
            att_s[0:NEW, g * HD : (g + 1) * HD] = out[g * NEW : (g + 1) * NEW, :]

    split_product(att_s[...].astype(BF16), w_out, keep, send)


def pair_kernel(keep, got, own, s1, s2, s3):
    x = place()[0]
    own[...] = keep[x].astype(F32) + got[x].astype(F32)
    for d, out in ((1, s1), (2, s2), (3, s3)):
        to = (x + d) % 4
        out[...] = (keep[to].astype(F32) + got[to].astype(F32)).astype(BF16)


def core_sum_kernel(keep, got, out):
    out[...] = (keep[...].astype(F32) + got[...].astype(F32)).astype(BF16)


def residual_kernel(tok, own, r1, r2, r3, res, x_s):
    core = place()[1]
    for x in range(TEN // 2):
        at = pl.multiple_of((2 * x + core) * COLS, COLS)
        for r in range(REQ_DEV):
            x_s[r * NEW : (r + 1) * NEW, :] = tok[r, :, pl.ds(at, COLS)].astype(F32)
        total = own[x].astype(F32) + r1[x].astype(F32) + r2[x].astype(F32) + r3[x].astype(F32)
        res[x] = (x_s[...] + total).astype(BF16)


def mlp_kernel(mine, other, gain, w_gate, w_up, w_down, keep, send):
    core = place()[1]
    square = jnp.zeros((ROWS, 1), F32)
    for d in range(4):
        for blocks in (mine, other):
            v = blocks[d].astype(F32)
            square = square + jnp.sum(v * v, axis=1, keepdims=True)
    inverse = lax.rsqrt(square * (1.0 / D) + EPSILON)
    gate = jnp.zeros((ROWS, FF_DEV), F32)
    up = jnp.zeros((ROWS, FF_DEV), F32)
    for d in range(4):
        for c, blocks in ((core, mine), (1 - core, other)):
            b = 2 * d + c
            at = pl.multiple_of(b * COLS, COLS)
            normed = (blocks[d].astype(F32) * inverse * gain[:, pl.ds(at, COLS)].astype(F32)).astype(BF16)
            gate = gate + nn_dot(normed, w_gate[pl.ds(at, COLS), :])
            up = up + nn_dot(normed, w_up[pl.ds(at, COLS), :])
    activated = (gate / (1.0 + jnp.exp(-gate)) * up).astype(BF16)
    split_product(activated, w_down, keep, send)


def final_kernel(res, own, r1, r2, r3, out):
    total = own[...] + r1[...].astype(F32) + r2[...].astype(F32) + r3[...].astype(F32)
    total = (res[place()[0]].astype(F32) + total).astype(BF16)
    for r in range(REQ_DEV):
        out[r] = total[r * NEW : (r + 1) * NEW, :]


def swap_core(v):
    return lax.ppermute(v, "tensor", [(i, i ^ 1) for i in range(TEN)])


def along_x(v, d):
    return lax.ppermute(v, "tensor", [(i, (i + 2 * d) % TEN) for i in range(TEN)])


def scatter_sum(keep, send):
    got = swap_core(send)
    block = sds((ROWS, COLS), BF16)
    own, s1, s2, s3 = call(pair_kernel, (sds((ROWS, COLS), F32), block, block, block), [VMEM, VMEM], [], 1)(keep, got)
    return own, along_x(s1, 1), along_x(s2, 2), along_x(s3, 3)


def per_device(
    tokens,
    lengths,
    page_request,
    page_block,
    k_cache,
    v_cache,
    attn_gain,
    w_query,
    w_key,
    w_value,
    w_out,
    mlp_gain,
    w_gate,
    w_up,
    w_down,
):
    half = np.arange(HD) % (HD // 2)
    inv = jnp.asarray((1.0 / ROPE_BASE ** (half * 2.0 / HD)).astype(np.float32).reshape(1, HD))
    k_cache = k_cache.reshape(SLOTS, PAGE, HD)
    v_cache = v_cache.reshape(SLOTS, PAGE, HD)
    dma = pltpu.SemaphoreType.DMA

    def in_hbm(*arrays):
        return tuple(pltpu.with_memory_space_constraint(a, pltpu.HBM) for a in arrays)

    q_pack, k_new, v_new, q_long, table = call(
        qkv_kernel,
        (
            sds((REQ_DEV // 2 * 32, HD), F32),
            sds((ROWS, HD), BF16),
            sds((ROWS, HD), BF16),
            sds((SEQ, 16, HD), BF16),
            pltpu.SMEM((8, SLOTS), jnp.int32),
        ),
        [HBM] * 9,
        [
            pltpu.SMEM(lengths.shape, jnp.int32),
            pltpu.VMEM((1, SLOTS), jnp.int32),
            pltpu.VMEM((1, SLOTS), jnp.int32),
            pltpu.VMEM(tokens.shape, BF16),
            pltpu.VMEM((D,), BF16),
            pltpu.VMEM((1, HD), F32),
            pltpu.VMEM(w_query.shape, BF16),
            pltpu.VMEM(w_key.shape, BF16),
            pltpu.VMEM(w_value.shape, BF16),
            pltpu.VMEM((ROWS, D), F32),
            pltpu.VMEM((ROWS, HD), jnp.int32),
            pltpu.VMEM((16, HD), F32),
            pltpu.VMEM((8, SLOTS), jnp.int32),
            dma((11,)),
            dma(()),
        ],
        8,
        [VMEM] * 4 + [SMEM],
    )(*in_hbm(lengths, page_request, page_block, tokens, attn_gain, inv, w_query, w_key, w_value))

    q_all = lax.all_to_all(q_long, "seq", 0, 0, tiled=True)

    column = pltpu.VMEM((16, HD), F32)
    longs = pltpu.VMEM((LONGS, 16, HD), F32)
    pairs = REQ_DEV // 2
    att, part0, part = call(
        attend_kernel,
        (sds((ROWS, QCOLS), F32), sds((16, HD), F32), sds((SEQ, 16, HD), BF16)),
        [SMEM] + [VMEM] * 5 + [HBM],
        [
            pltpu.VMEM(v_cache.shape, BF16),
            pltpu.VMEM((pairs, 32, ROWS), F32),
            pltpu.VMEM((pairs, 32, CHUNK * PAGE), F32),
            pltpu.VMEM((pairs, 32, HD), F32),
            pltpu.VMEM((pairs, 32, HD), F32),
            pltpu.VMEM((pairs, 32, HD), F32),
            pltpu.VMEM((ROWS, QCOLS), F32),
            column,
            column,
            column,
            pltpu.VMEM((2 * SLOTS // CHUNK, 16, CHUNK * PAGE), F32),
            longs,
            longs,
            longs,
            dma(()),
        ],
        10,
    )(table, q_pack, k_new, v_new, q_all, k_cache, *in_hbm(v_cache))

    parts = lax.all_to_all(part, "seq", 0, 0, tiled=True)

    halves = (sds((TEN // 2, ROWS, COLS), BF16), sds((TEN // 2, ROWS, COLS), BF16))
    keep, send = call(
        out_kernel,
        halves,
        [VMEM] * 4,
        [pltpu.VMEM((ROWS, QCOLS), F32), pltpu.VMEM((SEQ, HD), F32), pltpu.VMEM((SEQ, HD), F32)],
        2,
    )(att, part0, parts, w_out)
    half = sds((TEN // 2, ROWS, COLS), BF16)
    own = call(core_sum_kernel, half, [VMEM] * 2, [], 1)(keep, swap_core(send))
    mine = call(
        residual_kernel, half, [VMEM] * 5, [pltpu.VMEM((ROWS, COLS), F32)], 1
    )(tokens, own, along_x(own, 1), along_x(own, 2), along_x(own, 3))
    other = swap_core(mine)

    keep, send = call(mlp_kernel, halves, [VMEM] * 6, [], 4)(mine, other, mlp_gain.reshape(1, D), w_gate, w_up, w_down)
    own, r1, r2, r3 = scatter_sum(keep, send)

    return call(final_kernel, sds((REQ_DEV, NEW, COLS), BF16), [VMEM] * 5, [], 1)(mine, own, r1, r2, r3)


def solution(mesh):
    placed = (
        P("seq", None, None),
        P(),
        P("seq"),
        P("seq"),
        P("seq", "tensor", None, None),
        P("seq", "tensor", None, None),
        P(),
        P(None, "tensor"),
        P(None, "tensor"),
        P(None, "tensor"),
        P("tensor", None),
        P(),
        P(None, "tensor"),
        P(None, "tensor"),
        P("tensor", None),
    )

    return jax.shard_map(per_device, mesh=mesh, in_specs=placed, out_specs=P("seq", None, "tensor"), check_vma=False)
```

profile of v0, /device:TPU:0, one launch (start us, length us, event | category | flops | bytes accessed | tf_op | source)
XLA Modules:
  0.0 65.2 jit_solution(16036218657671182024)
XLA Ops:
  0.0 0.0 copy-start
  0.0 4.5 %shard_map.154 = (f32[256,128]{1,0:T(8,128)S(1)}, bf16[64,128]{1,0:T(8,128)(2,1)S(1)}, bf16[64,128]{1,0:T(8,128)(2,1)S(1)}, bf16[16,16,128]{2,1,0:T(8,128)(2,1)S(1)}, s32[8,128]{1,0:T(8,128)S(4)}) custom-call(s32[256]{0:T(256)} %lengths_h.1, s32[128]{0:T(128)} %request_h.1, s32[128]{0:T(128)} %block_h.1, bf16[16,4,3072]{2,1,0:T(4,128)(2,1)} %tok.1, ...), custom_call_target="tpu_custom_call" | custom-call | tf_op jit(solution)/shard_map/pallas_call | solution.py:455
  4.5 15.6 %all_to_all.10.q_all = bf16[16,16,128]{2,1,0:T(8,128)(2,1)S(1)} all-to-all(bf16[16,16,128]{2,1,0:T(8,128)(2,1)S(1)} %get-tuple-element.25), channel_id=1, replica_groups=mesh['seq'=16,'tensor'=8] {'seq'}, dimensions={0} | all-to-all | bytes 131072 | tf_op jit(solution)/shard_map/all_to_all | solution.py:486
  20.1 0.0 copy-done
  20.1 0.0 copy-start.4
  20.1 0.0 copy-start.5
  20.1 0.0 copy-start.2
  20.1 0.0 copy-start.3
  20.1 4.5 %shard_map.155 = (f32[64,384]{1,0:T(8,128)S(1)}, f32[16,128]{1,0:T(8,128)S(1)}, bf16[16,16,128]{2,1,0:T(8,128)(2,1)S(1)}) custom-call(s32[8,128]{1,0:T(8,128)S(4)} %get-tuple-element.21.table, f32[256,128]{1,0:T(8,128)S(1)} %get-tuple-element.22.q_pack, bf16[64,128]{1,0:T(8,128)(2,1)S(1)} %get-tuple-element.23.k_new, ...), custom_call_target="tpu_custom_call" | custom-call | tf_op jit(solution)/shard_map/pallas_call | solution.py:491
  24.6 0.0 copy-start.6
  24.6 0.0 copy-start.1
  24.7 11.1 %all_to_all.11.parts = bf16[16,16,128]{2,1,0:T(8,128)(2,1)S(1)} all-to-all(bf16[16,16,128]{2,1,0:T(8,128)(2,1)S(1)} %get-tuple-element.28), channel_id=1, replica_groups=mesh['seq'=16,'tensor'=8] {'seq'}, dimensions={0} | all-to-all | bytes 131072 | tf_op jit(solution)/shard_map/all_to_all | solution.py:515
  35.7 0.0 copy-done.4
  35.7 0.8 %shard_map.156 = (bf16[4,64,384]{2,1,0:T(8,128)(2,1)S(1)}, bf16[4,64,384]{2,1,0:T(8,128)(2,1)S(1)}) custom-call(f32[64,384]{1,0:T(8,128)S(1)} %get-tuple-element.26.att, f32[16,128]{1,0:T(8,128)S(1)} %get-tuple-element.27.part0, bf16[16,16,128]{2,1,0:T(8,128)(2,1)S(1)} %all_to_all.11.parts, bf16[384,3072]{1,0:T(8,128)(2,1)S(1)} %copy-done.4), custom_call_target="tpu_custom_call" | custom-call | tf_op jit(solution)/shard_map/pallas_call | solution.py:518
  36.5 0.1 collective-permute-start
  36.6 1.4 %collective-permute-done.got = bf16[4,64,384]{2,1,0:T(8,128)(2,1)S(1)} collective-permute-done((bf16[4,64,384]{2,1,0:T(8,128)(2,1)S(1)}, bf16[4,64,384]{2,1,0:T(8,128)(2,1)S(1)}, u32[]{:S(2)}, u32[]{:S(2)}) %collective-permute-start) | collective-permute-done | bytes 196640 | tf_op jit(solution)/shard_map/ppermute | solution.py:415
  38.0 0.1 shard_map.157.own
  38.1 1.6 %collective-permute-start.1 = (bf16[4,64,384]{2,1,0:T(8,128)(2,1)S(1)}, bf16[4,64,384]{2,1,0:T(8,128)(2,1)S(1)}, u32[]{:S(2)}, u32[]{:S(2)}) collective-permute-start(bf16[4,64,384]{2,1,0:T(8,128)(2,1)S(1)} %shard_map.157.own), channel_id=1, source_target_pairs={{0,2},{1,3},{2,4},{3,5},{4,6},{5,7},{6,0},{7,1},{8,10},{9,11},{10,... | collective-permute-start | bytes 589832 | tf_op jit(solution)/shard_map/ppermute | solution.py:419
  39.6 2.7 %collective-permute-start.2 = (bf16[4,64,384]{2,1,0:T(8,128)(2,1)S(1)}, bf16[4,64,384]{2,1,0:T(8,128)(2,1)S(1)}, u32[]{:S(2)}, u32[]{:S(2)}) collective-permute-start(bf16[4,64,384]{2,1,0:T(8,128)(2,1)S(1)} %shard_map.157.own), channel_id=1, source_target_pairs={{0,4},{1,5},{2,6},{3,7},{4,0},{5,1},{6,2},{7,3},{8,12},{9,13},{10,... | collective-permute-start | bytes 589832 | tf_op jit(solution)/shard_map/ppermute | solution.py:419
  42.3 1.4 %collective-permute-start.3 = (bf16[4,64,384]{2,1,0:T(8,128)(2,1)S(1)}, bf16[4,64,384]{2,1,0:T(8,128)(2,1)S(1)}, u32[]{:S(2)}, u32[]{:S(2)}) collective-permute-start(bf16[4,64,384]{2,1,0:T(8,128)(2,1)S(1)} %shard_map.157.own), channel_id=1, source_target_pairs={{0,6},{1,7},{2,0},{3,1},{4,2},{5,3},{6,4},{7,5},{8,14},{9,15},{10,... | collective-permute-start | bytes 589832 | tf_op jit(solution)/shard_map/ppermute | solution.py:419
  43.8 2.5 %collective-permute-done.1.r1 = bf16[4,64,384]{2,1,0:T(8,128)(2,1)S(1)} collective-permute-done((bf16[4,64,384]{2,1,0:T(8,128)(2,1)S(1)}, bf16[4,64,384]{2,1,0:T(8,128)(2,1)S(1)}, u32[]{:S(2)}, u32[]{:S(2)}) %collective-permute-start.1) | collective-permute-done | bytes 196640 | tf_op jit(solution)/shard_map/ppermute | solution.py:419
  46.3 5.2 %collective-permute-done.2.r2 = bf16[4,64,384]{2,1,0:T(8,128)(2,1)S(1)} collective-permute-done((bf16[4,64,384]{2,1,0:T(8,128)(2,1)S(1)}, bf16[4,64,384]{2,1,0:T(8,128)(2,1)S(1)}, u32[]{:S(2)}, u32[]{:S(2)}) %collective-permute-start.2) | collective-permute-done | bytes 196640 | tf_op jit(solution)/shard_map/ppermute | solution.py:419
  51.5 0.0 collective-permute-done.3.r3
  51.5 0.0 copy-done.5
  51.5 0.1 shard_map.158.mine.res
  51.6 0.1 collective-permute-start.4
  51.7 0.0 copy-done.6
  51.8 1.4 %collective-permute-done.4.other = bf16[4,64,384]{2,1,0:T(8,128)(2,1)S(1)} collective-permute-done((bf16[4,64,384]{2,1,0:T(8,128)(2,1)S(1)}, bf16[4,64,384]{2,1,0:T(8,128)(2,1)S(1)}, u32[]{:S(2)}, u32[]{:S(2)}) %collective-permute-start.4) | collective-permute-done | bytes 196640 | tf_op jit(solution)/shard_map/ppermute | solution.py:415
  53.2 0.0 copy-done.2
  53.2 0.0 copy-done.3
  53.2 0.0 copy-done.1
  53.2 1.9 %shard_map.159 = (bf16[4,64,384]{2,1,0:T(8,128)(2,1)S(1)}, bf16[4,64,384]{2,1,0:T(8,128)(2,1)S(1)}) custom-call(bf16[4,64,384]{2,1,0:T(8,128)(2,1)S(1)} %shard_map.158.mine.res, bf16[4,64,384]{2,1,0:T(8,128)(2,1)S(1)} %collective-permute-done.4.other, bf16[1,3072]{1,0:T(2,128)(2,1)S(1)} %reshape.11.gain, bf16[3072,512]{1,0:T(8,128)(2,1)S(1)} %copy-done.1, ...), custom_call_target="tpu_custom_call" | custom-call | tf_op jit(solution)/shard_map/pallas_call | solution.py:532
  55.1 0.2 collective-permute-start.5
  55.3 1.3 %collective-permute-done.5.got = bf16[4,64,384]{2,1,0:T(8,128)(2,1)S(1)} collective-permute-done((bf16[4,64,384]{2,1,0:T(8,128)(2,1)S(1)}, bf16[4,64,384]{2,1,0:T(8,128)(2,1)S(1)}, u32[]{:S(2)}, u32[]{:S(2)}) %collective-permute-start.5) | collective-permute-done | bytes 196640 | tf_op jit(solution)/shard_map/ppermute | solution.py:415
  56.7 1.4 %collective-permute-start.6 = (bf16[64,384]{1,0:T(8,128)(2,1)S(1)}, bf16[64,384]{1,0:T(8,128)(2,1)S(1)}, u32[]{:S(2)}, u32[]{:S(2)}) collective-permute-start(bf16[64,384]{1,0:T(8,128)(2,1)S(1)} %get-tuple-element.34), channel_id=1, source_target_pairs={{0,2},{1,3},{2,4},{3,5},{4,6},{5,7},{6,0},{7,1},{8,10},{9,11},{10,... | collective-permute-start | bytes 147464 | tf_op jit(solution)/shard_map/ppermute | solution.py:419
  58.1 2.4 %collective-permute-start.7 = (bf16[64,384]{1,0:T(8,128)(2,1)S(1)}, bf16[64,384]{1,0:T(8,128)(2,1)S(1)}, u32[]{:S(2)}, u32[]{:S(2)}) collective-permute-start(bf16[64,384]{1,0:T(8,128)(2,1)S(1)} %get-tuple-element.35), channel_id=1, source_target_pairs={{0,4},{1,5},{2,6},{3,7},{4,0},{5,1},{6,2},{7,3},{8,12},{9,13},{10,... | collective-permute-start | bytes 147464 | tf_op jit(solution)/shard_map/ppermute | solution.py:419
  60.5 1.5 %collective-permute-start.8 = (bf16[64,384]{1,0:T(8,128)(2,1)S(1)}, bf16[64,384]{1,0:T(8,128)(2,1)S(1)}, u32[]{:S(2)}, u32[]{:S(2)}) collective-permute-start(bf16[64,384]{1,0:T(8,128)(2,1)S(1)} %get-tuple-element.36), channel_id=1, source_target_pairs={{0,6},{1,7},{2,0},{3,1},{4,2},{5,3},{6,4},{7,5},{8,14},{9,15},{10,... | collective-permute-start | bytes 147464 | tf_op jit(solution)/shard_map/ppermute | solution.py:419
  62.0 0.0 collective-permute-done.6.r1
  62.0 1.6 %collective-permute-done.7.r2 = bf16[64,384]{1,0:T(8,128)(2,1)S(1)} collective-permute-done((bf16[64,384]{1,0:T(8,128)(2,1)S(1)}, bf16[64,384]{1,0:T(8,128)(2,1)S(1)}, u32[]{:S(2)}, u32[]{:S(2)}) %collective-permute-start.7) | collective-permute-done | bytes 49184 | tf_op jit(solution)/shard_map/ppermute | solution.py:419
  63.7 0.9 %collective-permute-done.8.r3 = bf16[64,384]{1,0:T(8,128)(2,1)S(1)} collective-permute-done((bf16[64,384]{1,0:T(8,128)(2,1)S(1)}, bf16[64,384]{1,0:T(8,128)(2,1)S(1)}, u32[]{:S(2)}, u32[]{:S(2)}) %collective-permute-start.8) | collective-permute-done | bytes 49184 | tf_op jit(solution)/shard_map/ppermute | solution.py:419
  64.6 0.7 %shard_map.161 = bf16[16,4,384]{2,1,0:T(4,128)(2,1)} custom-call(bf16[4,64,384]{2,1,0:T(8,128)(2,1)S(1)} %shard_map.158.mine.res, f32[64,384]{1,0:T(8,128)S(1)} %get-tuple-element.33.own, bf16[64,384]{1,0:T(8,128)(2,1)S(1)} %collective-permute-done.6.r1, bf16[64,384]{1,0:T(8,128)(2,1)S(1)} %collective-permute-done.7.r2, ...), custom_call_target="tpu_custom_call" | custom-call | tf_op jit(solution)/shard_map/pallas_call | solution.py:535
  (2 shorter events, 0.1 us)
Async XLA Ops:
  0.0 20.1 %copy-start = (bf16[128,1,128,128]{3,2,1,0:T(8,128)(2,1)S(1)}, bf16[128,1,128,128]{3,2,1,0:T(8,128)(2,1)}, u32[]{:S(2)}) copy-start(bf16[128,1,128,128]{3,2,1,0:T(8,128)(2,1)} %param.20) | copy-start | bytes 12582916
  20.1 15.6 %copy-start.4 = (bf16[384,3072]{1,0:T(8,128)(2,1)S(1)}, bf16[384,3072]{1,0:T(8,128)(2,1)}, u32[]{:S(2)}) copy-start(bf16[384,3072]{1,0:T(8,128)(2,1)} %w_out.1) | copy-start | bytes 7077892
  20.1 31.4 %copy-start.5 = (bf16[16,4,3072]{2,1,0:T(4,128)(2,1)S(1)}, bf16[16,4,3072]{2,1,0:T(4,128)(2,1)}, u32[]{:S(2)}) copy-start(bf16[16,4,3072]{2,1,0:T(4,128)(2,1)} %tok.1) | copy-start | bytes 1179652
  20.1 33.1 %copy-start.2 = (bf16[3072,512]{1,0:T(8,128)(2,1)S(1)}, bf16[3072,512]{1,0:T(8,128)(2,1)}, u32[]{:S(2)}) copy-start(bf16[3072,512]{1,0:T(8,128)(2,1)} %w_up.1) | copy-start | bytes 9437188
  20.1 33.0 %copy-start.3 = (bf16[512,3072]{1,0:T(8,128)(2,1)S(1)}, bf16[512,3072]{1,0:T(8,128)(2,1)}, u32[]{:S(2)}) copy-start(bf16[512,3072]{1,0:T(8,128)(2,1)} %w_down.1) | copy-start | bytes 9437188
  24.6 27.1 %copy-start.6 = (bf16[3072]{0:T(1024)(128)(2,1)S(1)}, bf16[3072]{0:T(1024)(128)(2,1)}, u32[]{:S(2)}) copy-start(bf16[3072]{0:T(1024)(128)(2,1)} %param.27) | copy-start | bytes 18436
  24.6 28.5 %copy-start.1 = (bf16[3072,512]{1,0:T(8,128)(2,1)S(1)}, bf16[3072,512]{1,0:T(8,128)(2,1)}, u32[]{:S(2)}) copy-start(bf16[3072,512]{1,0:T(8,128)(2,1)} %w_gate.1) | copy-start | bytes 9437188
  36.5 1.5 %collective-permute-start = (bf16[4,64,384]{2,1,0:T(8,128)(2,1)S(1)}, bf16[4,64,384]{2,1,0:T(8,128)(2,1)S(1)}, u32[]{:S(2)}, u32[]{:S(2)}) collective-permute-start(bf16[4,64,384]{2,1,0:T(8,128)(2,1)S(1)} %get-tuple-element.30), channel_id=1, source_target_pairs={{0,1},{1,0},{2,3},{3,2},{4,5},{5,4},{6,7},{7,6},{8,9},{9,8},{10,11... | collective-permute-start | bytes 589832 | tf_op jit(solution)/shard_map/ppermute | solution.py:415
  38.1 8.2 %collective-permute-start.1 = (bf16[4,64,384]{2,1,0:T(8,128)(2,1)S(1)}, bf16[4,64,384]{2,1,0:T(8,128)(2,1)S(1)}, u32[]{:S(2)}, u32[]{:S(2)}) collective-permute-start(bf16[4,64,384]{2,1,0:T(8,128)(2,1)S(1)} %shard_map.157.own), channel_id=1, source_target_pairs={{0,2},{1,3},{2,4},{3,5},{4,6},{5,7},{6,0},{7,1},{8,10},{9,11},{10,... | collective-permute-start | bytes 589832 | tf_op jit(solution)/shard_map/ppermute | solution.py:419
  39.6 11.9 %collective-permute-start.2 = (bf16[4,64,384]{2,1,0:T(8,128)(2,1)S(1)}, bf16[4,64,384]{2,1,0:T(8,128)(2,1)S(1)}, u32[]{:S(2)}, u32[]{:S(2)}) collective-permute-start(bf16[4,64,384]{2,1,0:T(8,128)(2,1)S(1)} %shard_map.157.own), channel_id=1, source_target_pairs={{0,4},{1,5},{2,6},{3,7},{4,0},{5,1},{6,2},{7,3},{8,12},{9,13},{10,... | collective-permute-start | bytes 589832 | tf_op jit(solution)/shard_map/ppermute | solution.py:419
  42.3 9.1 %collective-permute-start.3 = (bf16[4,64,384]{2,1,0:T(8,128)(2,1)S(1)}, bf16[4,64,384]{2,1,0:T(8,128)(2,1)S(1)}, u32[]{:S(2)}, u32[]{:S(2)}) collective-permute-start(bf16[4,64,384]{2,1,0:T(8,128)(2,1)S(1)} %shard_map.157.own), channel_id=1, source_target_pairs={{0,6},{1,7},{2,0},{3,1},{4,2},{5,3},{6,4},{7,5},{8,14},{9,15},{10,... | collective-permute-start | bytes 589832 | tf_op jit(solution)/shard_map/ppermute | solution.py:419
  51.6 1.5 %collective-permute-start.4 = (bf16[4,64,384]{2,1,0:T(8,128)(2,1)S(1)}, bf16[4,64,384]{2,1,0:T(8,128)(2,1)S(1)}, u32[]{:S(2)}, u32[]{:S(2)}) collective-permute-start(bf16[4,64,384]{2,1,0:T(8,128)(2,1)S(1)} %shard_map.158.mine.res), channel_id=1, source_target_pairs={{0,1},{1,0},{2,3},{3,2},{4,5},{5,4},{6,7},{7,6},{8,9},{9,8},{10,11... | collective-permute-start | bytes 589832 | tf_op jit(solution)/shard_map/ppermute | solution.py:415
  55.1 1.5 %collective-permute-start.5 = (bf16[4,64,384]{2,1,0:T(8,128)(2,1)S(1)}, bf16[4,64,384]{2,1,0:T(8,128)(2,1)S(1)}, u32[]{:S(2)}, u32[]{:S(2)}) collective-permute-start(bf16[4,64,384]{2,1,0:T(8,128)(2,1)S(1)} %get-tuple-element.32), channel_id=1, source_target_pairs={{0,1},{1,0},{2,3},{3,2},{4,5},{5,4},{6,7},{7,6},{8,9},{9,8},{10,11... | collective-permute-start | bytes 589832 | tf_op jit(solution)/shard_map/ppermute | solution.py:415
  56.7 5.4 %collective-permute-start.6 = (bf16[64,384]{1,0:T(8,128)(2,1)S(1)}, bf16[64,384]{1,0:T(8,128)(2,1)S(1)}, u32[]{:S(2)}, u32[]{:S(2)}) collective-permute-start(bf16[64,384]{1,0:T(8,128)(2,1)S(1)} %get-tuple-element.34), channel_id=1, source_target_pairs={{0,2},{1,3},{2,4},{3,5},{4,6},{5,7},{6,0},{7,1},{8,10},{9,11},{10,... | collective-permute-start | bytes 147464 | tf_op jit(solution)/shard_map/ppermute | solution.py:419
  58.1 5.6 %collective-permute-start.7 = (bf16[64,384]{1,0:T(8,128)(2,1)S(1)}, bf16[64,384]{1,0:T(8,128)(2,1)S(1)}, u32[]{:S(2)}, u32[]{:S(2)}) collective-permute-start(bf16[64,384]{1,0:T(8,128)(2,1)S(1)} %get-tuple-element.35), channel_id=1, source_target_pairs={{0,4},{1,5},{2,6},{3,7},{4,0},{5,1},{6,2},{7,3},{8,12},{9,13},{10,... | collective-permute-start | bytes 147464 | tf_op jit(solution)/shard_map/ppermute | solution.py:419
  60.5 4.1 %collective-permute-start.8 = (bf16[64,384]{1,0:T(8,128)(2,1)S(1)}, bf16[64,384]{1,0:T(8,128)(2,1)S(1)}, u32[]{:S(2)}, u32[]{:S(2)}) collective-permute-start(bf16[64,384]{1,0:T(8,128)(2,1)S(1)} %get-tuple-element.36), channel_id=1, source_target_pairs={{0,6},{1,7},{2,0},{3,1},{4,2},{5,3},{6,4},{7,5},{8,14},{9,15},{10,... | collective-permute-start | bytes 147464 | tf_op jit(solution)/shard_map/ppermute | solution.py:419
where the time goes:
time: 65.4 us; the launch traced here: 65.2 us
  blocking collectives  26.7 us (41%)
  waiting for transfers between devices  14.4 us (22%)
  Pallas kernels  12.5 us (19%)
  starting transfers between devices  11.4 us (17%)
    all_to_all x1, blocking collectives, per_device(): q_all = lax.all_to_all(q_long, 'seq', 0, 0, tiled=True)  15.6 us
    all_to_all x1, blocking collectives, per_device(): parts = lax.all_to_all(part, 'seq', 0, 0, tiled=True)  11.1 us
    ppermute x6, starting transfers between devices, along_x(): lax.ppermute(v, 'tensor', [(i, (i + 2 * d) % TEN) for i in range(TEN)])  11.1 us
    ppermute x6, waiting for transfers between devices, along_x(): lax.ppermute(v, 'tensor', [(i, (i + 2 * d) % TEN) for i in range(TEN)])  10.2 us
    pallas_call x1, Pallas kernels, per_device(): call(attend_kernel, (sds((ROWS, QCOLS), F32), sds((16, HD), F32), sds((SE...  4.49 us
    pallas_call x1, Pallas kernels, per_device(): call(qkv_kernel, (sds((REQ_DEV // 2 * 32, HD), F32), sds((ROWS, HD), BF16...  4.46 us
    ppermute x3, waiting for transfers between devices, swap_core(): return lax.ppermute(v, 'tensor', [(i, i ^ 1) for i in range(TEN)])  4.14 us
    pallas_call x1, Pallas kernels, per_device(): call(mlp_kernel, halves, [VMEM] * 6, [], 4)  1.91 us
  transfers between devices with their start and end apart: 9, of which 7 were waited for; matrix products, arithmetic and copies ran while one was open for 0% of the time, Pallas kernels for 0%

commit v1 on v0

--- a/solution.py
+++ b/solution.py
@@ -318,17 +318,17 @@
     return tensor // 2, tensor % 2
 
 
-def split_product(a, w, keep, send):
-    core = place()[1]
-    for x in range(TEN // 2):
-        at = pl.multiple_of((2 * x + 1 - core) * COLS, COLS)
-        send[x] = nn_dot(a, w[:, pl.ds(at, COLS)]).astype(BF16)
+def half_product(a, w, core, out):
     for x in range(TEN // 2):
         at = pl.multiple_of((2 * x + core) * COLS, COLS)
-        keep[x] = nn_dot(a, w[:, pl.ds(at, COLS)]).astype(keep.dtype)
-
-
-def out_kernel(att, part0, parts, w_out, keep, send, att_s, m_s, l_s):
+        out[x] = nn_dot(a, w[:, pl.ds(at, COLS)]).astype(BF16)
+
+
+def keep_kernel(a, w, keep):
+    half_product(a[...], w, place()[1], keep)
+
+
+def out_kernel(att, part0, parts, w_out, full, send, att_s, m_s, l_s):
     att_s[...] = att[...]
 
     @pl.when(lax.axis_index("seq") % 2 == 0)
@@ -358,7 +358,8 @@
         for g in range(G):
             att_s[0:NEW, g * HD : (g + 1) * HD] = out[g * NEW : (g + 1) * NEW, :]
 
-    split_product(att_s[...].astype(BF16), w_out, keep, send)
+    full[...] = att_s[...].astype(BF16)
+    half_product(full[...], w_out, 1 - place()[1], send)
 
 
 def pair_kernel(keep, got, own, s1, s2, s3):
@@ -383,25 +384,39 @@
         res[x] = (x_s[...] + total).astype(BF16)
 
 
-def mlp_kernel(mine, other, gain, w_gate, w_up, w_down, keep, send):
+def half_gate(blocks, core, gain_s, w_gate, w_up, gate, up, square):
+    for x in range(TEN // 2):
+        at = pl.multiple_of((2 * x + core) * COLS, COLS)
+        v = blocks[x].astype(F32)
+        square = square + jnp.sum(v * v, axis=1, keepdims=True)
+        scaled = (v * gain_s[:, pl.ds(at, COLS)]).astype(BF16)
+        gate = gate + nn_dot(scaled, w_gate[pl.ds(at, COLS), :])
+        up = up + nn_dot(scaled, w_up[pl.ds(at, COLS), :])
+    return gate, up, square
+
+
+def near_kernel(mine, gain, w_gate, w_up, gate, up, square, gain_s):
+    gain_s[...] = gain[...].astype(F32).reshape(1, D)
+    zero = jnp.zeros((ROWS, FF_DEV), F32)
+    g, u, q = half_gate(mine, place()[1], gain_s, w_gate, w_up, zero, zero, jnp.zeros((ROWS, 1), F32))
+    gate[...] = g
+    up[...] = u
+    square[...] = jnp.broadcast_to(q, (ROWS, HD))
+
+
+def far_kernel(other, gain, gate, up, square, w_gate, w_up, w_down, act, send, gain_s):
     core = place()[1]
-    square = jnp.zeros((ROWS, 1), F32)
-    for d in range(4):
-        for blocks in (mine, other):
-            v = blocks[d].astype(F32)
-            square = square + jnp.sum(v * v, axis=1, keepdims=True)
-    inverse = lax.rsqrt(square * (1.0 / D) + EPSILON)
-    gate = jnp.zeros((ROWS, FF_DEV), F32)
-    up = jnp.zeros((ROWS, FF_DEV), F32)
-    for d in range(4):
-        for c, blocks in ((core, mine), (1 - core, other)):
-            b = 2 * d + c
-            at = pl.multiple_of(b * COLS, COLS)
-            normed = (blocks[d].astype(F32) * inverse * gain[:, pl.ds(at, COLS)].astype(F32)).astype(BF16)
-            gate = gate + nn_dot(normed, w_gate[pl.ds(at, COLS), :])
-            up = up + nn_dot(normed, w_up[pl.ds(at, COLS), :])
-    activated = (gate / (1.0 + jnp.exp(-gate)) * up).astype(BF16)
-    split_product(activated, w_down, keep, send)
+    gain_s[...] = gain[...].astype(F32).reshape(1, D)
+    g, u, q = half_gate(other, 1 - core, gain_s, w_gate, w_up, gate[...], up[...], square[:, 0:1])
+    inverse = lax.rsqrt(q * (1.0 / D) + EPSILON)
+    g = g * inverse
+    act[...] = (g / (1.0 + jnp.exp(-g)) * (u * inverse)).astype(BF16)
+    half_product(act[...], w_down, 1 - core, send)
+
+
+def fetch_kernel(after, wg_h, wu_h, wd_h, wg, wu, wd, sems):
+    for copy in start_all([(wg_h, wg), (wu_h, wu), (wd_h, wd)], sems):
+        copy.wait()
 
 
 def final_kernel(res, own, r1, r2, r3, out):
@@ -514,22 +529,36 @@
 
     parts = lax.all_to_all(part, "seq", 0, 0, tiled=True)
 
-    halves = (sds((TEN // 2, ROWS, COLS), BF16), sds((TEN // 2, ROWS, COLS), BF16))
-    keep, send = call(
+    half = sds((TEN // 2, ROWS, COLS), BF16)
+    full, send = call(
         out_kernel,
-        halves,
+        (sds((ROWS, QCOLS), BF16), half),
         [VMEM] * 4,
         [pltpu.VMEM((ROWS, QCOLS), F32), pltpu.VMEM((SEQ, HD), F32), pltpu.VMEM((SEQ, HD), F32)],
         2,
     )(att, part0, parts, w_out)
-    half = sds((TEN // 2, ROWS, COLS), BF16)
-    own = call(core_sum_kernel, half, [VMEM] * 2, [], 1)(keep, swap_core(send))
+    got = swap_core(send)
+    keep = call(keep_kernel, half, [VMEM] * 2, [], 1)(full, w_out)
+    own = call(core_sum_kernel, half, [VMEM] * 2, [], 1)(keep, got)
+    weights = (w_gate, w_up, w_down)
+    weights = call(
+        fetch_kernel, tuple(pltpu.VMEM(w.shape, BF16) for w in weights), [VMEM] + [HBM] * 3, [dma((3,))], 1
+    )(own, *in_hbm(*weights))
+    w_gate, w_up, w_down = (pltpu.with_memory_space_constraint(w, pltpu.VMEM) for w in weights)
     mine = call(
         residual_kernel, half, [VMEM] * 5, [pltpu.VMEM((ROWS, COLS), F32)], 1
     )(tokens, own, along_x(own, 1), along_x(own, 2), along_x(own, 3))
     other = swap_core(mine)
 
-    keep, send = call(mlp_kernel, halves, [VMEM] * 6, [], 4)(mine, other, mlp_gain.reshape(1, D), w_gate, w_up, w_down)
+    wide = sds((ROWS, FF_DEV), F32)
+    gain_s = pltpu.VMEM((1, D), F32)
+    gate, up, square = call(
+        near_kernel, (wide, wide, sds((ROWS, HD), F32)), [VMEM] * 4, [gain_s], 2
+    )(mine, mlp_gain, w_gate, w_up)
+    act, send = call(
+        far_kernel, (sds((ROWS, FF_DEV), BF16), half), [VMEM] * 8, [gain_s], 3
+    )(other, mlp_gain, gate, up, square, w_gate, w_up, w_down)
+    keep = call(keep_kernel, half, [VMEM] * 2, [], 1)(act, w_down)
     own, r1, r2, r3 = scatter_sum(keep, send)
 
     return call(final_kernel, sds((REQ_DEV, NEW, COLS), BF16), [VMEM] * 5, [], 1)(mine, own, r1, r2, r3)

time: 65.4 us -> 68.3 us (1.044)
  Pallas kernels: 12.5 us -> 16.6 us
  starting transfers between devices: 11.4 us -> 8.76 us
  waiting for transfers between devices: 14.4 us -> 15.9 us
    pallas_call x3 -> x7, Pallas kernels: 2.71 us -> 6.83 us  [the longest x1 3.78 us: per_device(): call(fetch_kernel, tuple((pltpu.VMEM(w.shape, BF16) for w in weights)), [...]
    ppermute x6, waiting for transfers between devices: 10.2 us -> 14.1 us  [along_x(): lax.ppermute(v, 'tensor', [(i, (i + 2 * d) % TEN) for i in range(TEN)])]
    ppermute x6, starting transfers between devices: 11.1 us -> 8.01 us  [along_x(): lax.ppermute(v, 'tensor', [(i, (i + 2 * d) % TEN) for i in range(TEN)])]
    ppermute x3, waiting for transfers between devices: 4.14 us -> 1.78 us  [swap_core(): return lax.ppermute(v, 'tensor', [(i, i ^ 1) for i in range(TEN)])]
  transfers between devices with their start and end apart: 9 -> 9, of which waited for: 7 -> 7; matrix products, arithmetic and copies ran while one was open for 0% -> 0% of each run, Pallas kernels for 0% -> 8%
where the time goes in v1:
time: 68.3 us; the launch traced here: 68 us
  blocking collectives  26.6 us (39%)
  Pallas kernels  16.6 us (24%)
  waiting for transfers between devices  15.9 us (23%)
  starting transfers between devices  8.76 us (13%)
    all_to_all x1, blocking collectives, per_device(): q_all = lax.all_to_all(q_long, 'seq', 0, 0, tiled=True)  15.6 us
    ppermute x6, waiting for transfers between devices, along_x(): lax.ppermute(v, 'tensor', [(i, (i + 2 * d) % TEN) for i in range(TEN)])  14.1 us
    all_to_all x1, blocking collectives, per_device(): parts = lax.all_to_all(part, 'seq', 0, 0, tiled=True)  10.9 us
    ppermute x6, starting transfers between devices, along_x(): lax.ppermute(v, 'tensor', [(i, (i + 2 * d) % TEN) for i in range(TEN)])  8.01 us
    pallas_call x1, Pallas kernels, per_device(): call(attend_kernel, (sds((ROWS, QCOLS), F32), sds((16, HD), F32), sds((SE...  4.48 us
    pallas_call x1, Pallas kernels, per_device(): call(qkv_kernel, (sds((REQ_DEV // 2 * 32, HD), F32), sds((ROWS, HD), BF16...  4.46 us
    pallas_call x1, Pallas kernels, per_device(): call(fetch_kernel, tuple((pltpu.VMEM(w.shape, BF16) for w in weights)), [...  3.78 us
    ppermute x3, waiting for transfers between devices, swap_core(): return lax.ppermute(v, 'tensor', [(i, i ^ 1) for i in range(TEN)])  1.78 us
  transfers between devices with their start and end apart: 9, of which 7 were waited for; matrix products, arithmetic and copies ran while one was open for 0% of the time, Pallas kernels for 8%

profile of v1, /device:TPU:0, one launch (start us, length us, event | category | flops | bytes accessed | tf_op | source)
XLA Modules:
  0.0 68.0 jit_solution(8617425564142992554)
XLA Ops:
  0.0 0.0 copy-start.1
  0.0 4.5 %shard_map.154 = (f32[256,128]{1,0:T(8,128)S(1)}, bf16[64,128]{1,0:T(8,128)(2,1)S(1)}, bf16[64,128]{1,0:T(8,128)(2,1)S(1)}, bf16[16,16,128]{2,1,0:T(8,128)(2,1)S(1)}, s32[8,128]{1,0:T(8,128)S(4)}) custom-call(s32[256]{0:T(256)} %lengths_h.1, s32[128]{0:T(128)} %request_h.1, s32[128]{0:T(128)} %block_h.1, bf16[16,4,3072]{2,1,0:T(4,128)(2,1)} %tok.1, ...), custom_call_target="tpu_custom_call" | custom-call | tf_op jit(solution)/shard_map/pallas_call | solution.py:470
  4.5 15.6 %all_to_all.10.q_all = bf16[16,16,128]{2,1,0:T(8,128)(2,1)S(1)} all-to-all(bf16[16,16,128]{2,1,0:T(8,128)(2,1)S(1)} %get-tuple-element.31), channel_id=1, replica_groups=mesh['seq'=16,'tensor'=8] {'seq'}, dimensions={0} | all-to-all | bytes 131072 | tf_op jit(solution)/shard_map/all_to_all | solution.py:501
  20.1 0.0 copy-done.1
  20.1 0.0 copy-start
  20.1 4.5 %shard_map.155 = (f32[64,384]{1,0:T(8,128)S(1)}, f32[16,128]{1,0:T(8,128)S(1)}, bf16[16,16,128]{2,1,0:T(8,128)(2,1)S(1)}) custom-call(s32[8,128]{1,0:T(8,128)S(4)} %get-tuple-element.27.table, f32[256,128]{1,0:T(8,128)S(1)} %get-tuple-element.28.q_pack, bf16[64,128]{1,0:T(8,128)(2,1)S(1)} %get-tuple-element.29.k_new, ...), custom_call_target="tpu_custom_call" | custom-call | tf_op jit(solution)/shard_map/pallas_call | solution.py:506
  24.6 0.0 copy-start.2
  24.6 10.9 %all_to_all.11.parts = bf16[16,16,128]{2,1,0:T(8,128)(2,1)S(1)} all-to-all(bf16[16,16,128]{2,1,0:T(8,128)(2,1)S(1)} %get-tuple-element.34), channel_id=1, replica_groups=mesh['seq'=16,'tensor'=8] {'seq'}, dimensions={0} | all-to-all | bytes 131072 | tf_op jit(solution)/shard_map/all_to_all | solution.py:530
  35.5 0.0 copy-done
  35.5 0.6 shard_map.156
  36.1 0.1 collective-permute-start
  36.2 0.3 shard_map.157.keep
  36.6 1.1 %collective-permute-done.got = bf16[4,64,384]{2,1,0:T(8,128)(2,1)S(1)} collective-permute-done((bf16[4,64,384]{2,1,0:T(8,128)(2,1)S(1)}, bf16[4,64,384]{2,1,0:T(8,128)(2,1)S(1)}, u32[]{:S(2)}, u32[]{:S(2)}) %collective-permute-start) | collective-permute-done | bytes 196640 | tf_op jit(solution)/shard_map/ppermute | solution.py:430
  37.7 0.1 shard_map.158.own.after
  37.7 2.8 %collective-permute-start.3 = (bf16[4,64,384]{2,1,0:T(8,128)(2,1)S(1)}, bf16[4,64,384]{2,1,0:T(8,128)(2,1)S(1)}, u32[]{:S(2)}, u32[]{:S(2)}) collective-permute-start(bf16[4,64,384]{2,1,0:T(8,128)(2,1)S(1)} %shard_map.158.own.after), channel_id=1, source_target_pairs={{0,6},{1,7},{2,0},{3,1},{4,2},{5,3},{6,4},{7,5},{8,14},{9,15},{10,... | collective-permute-start | bytes 589832 | tf_op jit(solution)/shard_map/ppermute | solution.py:434
  40.5 0.8 %collective-permute-start.2 = (bf16[4,64,384]{2,1,0:T(8,128)(2,1)S(1)}, bf16[4,64,384]{2,1,0:T(8,128)(2,1)S(1)}, u32[]{:S(2)}, u32[]{:S(2)}) collective-permute-start(bf16[4,64,384]{2,1,0:T(8,128)(2,1)S(1)} %shard_map.158.own.after), channel_id=1, source_target_pairs={{0,4},{1,5},{2,6},{3,7},{4,0},{5,1},{6,2},{7,3},{8,12},{9,13},{10,... | collective-permute-start | bytes 589832 | tf_op jit(solution)/shard_map/ppermute | solution.py:434
  41.3 0.9 %collective-permute-start.1 = (bf16[4,64,384]{2,1,0:T(8,128)(2,1)S(1)}, bf16[4,64,384]{2,1,0:T(8,128)(2,1)S(1)}, u32[]{:S(2)}, u32[]{:S(2)}) collective-permute-start(bf16[4,64,384]{2,1,0:T(8,128)(2,1)S(1)} %shard_map.158.own.after), channel_id=1, source_target_pairs={{0,2},{1,3},{2,4},{3,5},{4,6},{5,7},{6,0},{7,1},{8,10},{9,11},{10,... | collective-permute-start | bytes 589832 | tf_op jit(solution)/shard_map/ppermute | solution.py:434
  42.2 7.0 %collective-permute-done.3.r3 = bf16[4,64,384]{2,1,0:T(8,128)(2,1)S(1)} collective-permute-done((bf16[4,64,384]{2,1,0:T(8,128)(2,1)S(1)}, bf16[4,64,384]{2,1,0:T(8,128)(2,1)S(1)}, u32[]{:S(2)}, u32[]{:S(2)}) %collective-permute-start.3) | collective-permute-done | bytes 196640 | tf_op jit(solution)/shard_map/ppermute | solution.py:434
  49.2 0.6 collective-permute-done.2.r2
  49.9 3.1 %collective-permute-done.1.r1 = bf16[4,64,384]{2,1,0:T(8,128)(2,1)S(1)} collective-permute-done((bf16[4,64,384]{2,1,0:T(8,128)(2,1)S(1)}, bf16[4,64,384]{2,1,0:T(8,128)(2,1)S(1)}, u32[]{:S(2)}, u32[]{:S(2)}) %collective-permute-start.1) | collective-permute-done | bytes 196640 | tf_op jit(solution)/shard_map/ppermute | solution.py:434
  52.9 0.0 copy-done.2
  52.9 0.2 shard_map.159.mine.res
  53.1 0.0 copy-start.3
  53.1 0.1 collective-permute-start.4
  53.2 3.8 %shard_map.160 = (bf16[3072,512]{1,0:T(8,128)(2,1)S(1)}, bf16[3072,512]{1,0:T(8,128)(2,1)S(1)}, bf16[512,3072]{1,0:T(8,128)(2,1)S(1)}) custom-call(bf16[4,64,384]{2,1,0:T(8,128)(2,1)S(1)} %shard_map.158.own.after, bf16[3072,512]{1,0:T(8,128)(2,1)} %wg_h.1, bf16[3072,512]{1,0:T(8,128)(2,1)} %wu_h.1, bf16[512,3072]{1,0:T(8,128)(2,1)} %wd_h.1), custom_call_target="tpu_custom_call" | custom-call | tf_op jit(solution)/shard_map/pallas_call | solution.py:544
  57.0 0.0 copy-done.3
  57.0 0.7 %shard_map.161 = (f32[64,512]{1,0:T(8,128)S(1)}, f32[64,512]{1,0:T(8,128)S(1)}, f32[64,128]{1,0:T(8,128)S(1)}) custom-call(bf16[4,64,384]{2,1,0:T(8,128)(2,1)S(1)} %shard_map.159.mine.res, bf16[3072]{0:T(1024)(128)(2,1)S(1)} %copy-done.3, bf16[3072,512]{1,0:T(8,128)(2,1)S(1)} %get-tuple-element.37.w_gate, bf16[3072,512]{1,0:T(8,128)(2,1)S(1)} %get-tuple-element.38.w_up), custom_call_target="tpu_custom_call" | custom-call | tf_op jit(solution)/shard_map/pallas_call | solution.py:555
  57.7 0.0 collective-permute-done.4.other
  57.7 1.0 %shard_map.162 = (bf16[64,512]{1,0:T(8,128)(2,1)S(1)}, bf16[4,64,384]{2,1,0:T(8,128)(2,1)S(1)}) custom-call(bf16[4,64,384]{2,1,0:T(8,128)(2,1)S(1)} %collective-permute-done.4.other, bf16[3072]{0:T(1024)(128)(2,1)S(1)} %copy-done.3, f32[64,512]{1,0:T(8,128)S(1)} %get-tuple-element.39.gate, f32[64,512]{1,0:T(8,128)S(1)} %get-tuple-element.40.up, ...), custom_call_target="tpu_custom_call" | custom-call | tf_op jit(solution)/shard_map/pallas_call | solution.py:558
  58.7 0.6 collective-permute-start.5
  59.3 0.4 shard_map.163.keep
  59.7 0.7 %collective-permute-done.5.got = bf16[4,64,384]{2,1,0:T(8,128)(2,1)S(1)} collective-permute-done((bf16[4,64,384]{2,1,0:T(8,128)(2,1)S(1)}, bf16[4,64,384]{2,1,0:T(8,128)(2,1)S(1)}, u32[]{:S(2)}, u32[]{:S(2)}) %collective-permute-start.5) | collective-permute-done | bytes 196640 | tf_op jit(solution)/shard_map/ppermute | solution.py:430
  60.4 0.1 collective-permute-start.6
  60.5 2.1 %collective-permute-start.7 = (bf16[64,384]{1,0:T(8,128)(2,1)S(1)}, bf16[64,384]{1,0:T(8,128)(2,1)S(1)}, u32[]{:S(2)}, u32[]{:S(2)}) collective-permute-start(bf16[64,384]{1,0:T(8,128)(2,1)S(1)} %get-tuple-element.47), channel_id=1, source_target_pairs={{0,4},{1,5},{2,6},{3,7},{4,0},{5,1},{6,2},{7,3},{8,12},{9,13},{10,... | collective-permute-start | bytes 147464 | tf_op jit(solution)/shard_map/ppermute | solution.py:434
  62.6 1.4 %collective-permute-start.8 = (bf16[64,384]{1,0:T(8,128)(2,1)S(1)}, bf16[64,384]{1,0:T(8,128)(2,1)S(1)}, u32[]{:S(2)}, u32[]{:S(2)}) collective-permute-start(bf16[64,384]{1,0:T(8,128)(2,1)S(1)} %get-tuple-element.48), channel_id=1, source_target_pairs={{0,6},{1,7},{2,0},{3,1},{4,2},{5,3},{6,4},{7,5},{8,14},{9,15},{10,... | collective-permute-start | bytes 147464 | tf_op jit(solution)/shard_map/ppermute | solution.py:434
  63.9 2.8 %collective-permute-done.6.r1 = bf16[64,384]{1,0:T(8,128)(2,1)S(1)} collective-permute-done((bf16[64,384]{1,0:T(8,128)(2,1)S(1)}, bf16[64,384]{1,0:T(8,128)(2,1)S(1)}, u32[]{:S(2)}, u32[]{:S(2)}) %collective-permute-start.6) | collective-permute-done | bytes 49184 | tf_op jit(solution)/shard_map/ppermute | solution.py:434
  66.8 0.0 collective-permute-done.7.r2
  66.8 0.6 collective-permute-done.8.r3
  67.3 0.7 shard_map.165
  (1 shorter events, 0.0 us)
Async XLA Ops:
  0.0 20.1 %copy-start.1 = (bf16[128,1,128,128]{3,2,1,0:T(8,128)(2,1)S(1)}, bf16[128,1,128,128]{3,2,1,0:T(8,128)(2,1)}, u32[]{:S(2)}) copy-start(bf16[128,1,128,128]{3,2,1,0:T(8,128)(2,1)} %param.20) | copy-start | bytes 12582916
  20.1 15.4 %copy-start = (bf16[384,3072]{1,0:T(8,128)(2,1)S(1)}, bf16[384,3072]{1,0:T(8,128)(2,1)}, u32[]{:S(2)}) copy-start(bf16[384,3072]{1,0:T(8,128)(2,1)} %w.1) | copy-start | bytes 7077892
  24.6 28.3 %copy-start.2 = (bf16[16,4,3072]{2,1,0:T(4,128)(2,1)S(1)}, bf16[16,4,3072]{2,1,0:T(4,128)(2,1)}, u32[]{:S(2)}) copy-start(bf16[16,4,3072]{2,1,0:T(4,128)(2,1)} %tok.1) | copy-start | bytes 1179652
  36.1 1.5 %collective-permute-start = (bf16[4,64,384]{2,1,0:T(8,128)(2,1)S(1)}, bf16[4,64,384]{2,1,0:T(8,128)(2,1)S(1)}, u32[]{:S(2)}, u32[]{:S(2)}) collective-permute-start(bf16[4,64,384]{2,1,0:T(8,128)(2,1)S(1)} %get-tuple-element.36), channel_id=1, source_target_pairs={{0,1},{1,0},{2,3},{3,2},{4,5},{5,4},{6,7},{7,6},{8,9},{9,8},{10,11... | collective-permute-start | bytes 589832 | tf_op jit(solution)/shard_map/ppermute | solution.py:430
  37.7 11.5 %collective-permute-start.3 = (bf16[4,64,384]{2,1,0:T(8,128)(2,1)S(1)}, bf16[4,64,384]{2,1,0:T(8,128)(2,1)S(1)}, u32[]{:S(2)}, u32[]{:S(2)}) collective-permute-start(bf16[4,64,384]{2,1,0:T(8,128)(2,1)S(1)} %shard_map.158.own.after), channel_id=1, source_target_pairs={{0,6},{1,7},{2,0},{3,1},{4,2},{5,3},{6,4},{7,5},{8,14},{9,15},{10,... | collective-permute-start | bytes 589832 | tf_op jit(solution)/shard_map/ppermute | solution.py:434
  40.5 9.3 %collective-permute-start.2 = (bf16[4,64,384]{2,1,0:T(8,128)(2,1)S(1)}, bf16[4,64,384]{2,1,0:T(8,128)(2,1)S(1)}, u32[]{:S(2)}, u32[]{:S(2)}) collective-permute-start(bf16[4,64,384]{2,1,0:T(8,128)(2,1)S(1)} %shard_map.158.own.after), channel_id=1, source_target_pairs={{0,4},{1,5},{2,6},{3,7},{4,0},{5,1},{6,2},{7,3},{8,12},{9,13},{10,... | collective-permute-start | bytes 589832 | tf_op jit(solution)/shard_map/ppermute | solution.py:434
  41.3 11.6 %collective-permute-start.1 = (bf16[4,64,384]{2,1,0:T(8,128)(2,1)S(1)}, bf16[4,64,384]{2,1,0:T(8,128)(2,1)S(1)}, u32[]{:S(2)}, u32[]{:S(2)}) collective-permute-start(bf16[4,64,384]{2,1,0:T(8,128)(2,1)S(1)} %shard_map.158.own.after), channel_id=1, source_target_pairs={{0,2},{1,3},{2,4},{3,5},{4,6},{5,7},{6,0},{7,1},{8,10},{9,11},{10,... | collective-permute-start | bytes 589832 | tf_op jit(solution)/shard_map/ppermute | solution.py:434
  53.1 3.9 %copy-start.3 = (bf16[3072]{0:T(1024)(128)(2,1)S(1)}, bf16[3072]{0:T(1024)(128)(2,1)}, u32[]{:S(2)}) copy-start(bf16[3072]{0:T(1024)(128)(2,1)} %gain.3) | copy-start | bytes 18436
  53.1 4.6 %collective-permute-start.4 = (bf16[4,64,384]{2,1,0:T(8,128)(2,1)S(1)}, bf16[4,64,384]{2,1,0:T(8,128)(2,1)S(1)}, u32[]{:S(2)}, u32[]{:S(2)}) collective-permute-start(bf16[4,64,384]{2,1,0:T(8,128)(2,1)S(1)} %shard_map.159.mine.res), channel_id=1, source_target_pairs={{0,1},{1,0},{2,3},{3,2},{4,5},{5,4},{6,7},{7,6},{8,9},{9,8},{10,11... | collective-permute-start | bytes 589832 | tf_op jit(solution)/shard_map/ppermute | solution.py:430
  58.7 1.6 %collective-permute-start.5 = (bf16[4,64,384]{2,1,0:T(8,128)(2,1)S(1)}, bf16[4,64,384]{2,1,0:T(8,128)(2,1)S(1)}, u32[]{:S(2)}, u32[]{:S(2)}) collective-permute-start(bf16[4,64,384]{2,1,0:T(8,128)(2,1)S(1)} %get-tuple-element.44), channel_id=1, source_target_pairs={{0,1},{1,0},{2,3},{3,2},{4,5},{5,4},{6,7},{7,6},{8,9},{9,8},{10,11... | collective-permute-start | bytes 589832 | tf_op jit(solution)/shard_map/ppermute | solution.py:430
  60.4 6.4 %collective-permute-start.6 = (bf16[64,384]{1,0:T(8,128)(2,1)S(1)}, bf16[64,384]{1,0:T(8,128)(2,1)S(1)}, u32[]{:S(2)}, u32[]{:S(2)}) collective-permute-start(bf16[64,384]{1,0:T(8,128)(2,1)S(1)} %get-tuple-element.46), channel_id=1, source_target_pairs={{0,2},{1,3},{2,4},{3,5},{4,6},{5,7},{6,0},{7,1},{8,10},{9,11},{10,... | collective-permute-start | bytes 147464 | tf_op jit(solution)/shard_map/ppermute | solution.py:434
  60.5 6.3 %collective-permute-start.7 = (bf16[64,384]{1,0:T(8,128)(2,1)S(1)}, bf16[64,384]{1,0:T(8,128)(2,1)S(1)}, u32[]{:S(2)}, u32[]{:S(2)}) collective-permute-start(bf16[64,384]{1,0:T(8,128)(2,1)S(1)} %get-tuple-element.47), channel_id=1, source_target_pairs={{0,4},{1,5},{2,6},{3,7},{4,0},{5,1},{6,2},{7,3},{8,12},{9,13},{10,... | collective-permute-start | bytes 147464 | tf_op jit(solution)/shard_map/ppermute | solution.py:434
  62.6 4.8 %collective-permute-start.8 = (bf16[64,384]{1,0:T(8,128)(2,1)S(1)}, bf16[64,384]{1,0:T(8,128)(2,1)S(1)}, u32[]{:S(2)}, u32[]{:S(2)}) collective-permute-start(bf16[64,384]{1,0:T(8,128)(2,1)S(1)} %get-tuple-element.48), channel_id=1, source_target_pairs={{0,6},{1,7},{2,0},{3,1},{4,2},{5,3},{6,4},{7,5},{8,14},{9,15},{10,... | collective-permute-start | bytes 147464 | tf_op jit(solution)/shard_map/ppermute | solution.py:434

commit v2 on v1

--- a/solution.py
+++ b/solution.py
@@ -28,6 +28,7 @@
 COLS = D // TEN
 FF_DEV = 512
 SLOTS = 128
+LANES = 16
 LONG_STEP = 32
 LONGS = 8
 SHORT_BLK = 4
@@ -78,7 +79,7 @@
 def qkv_kernel(
     lengths_h, request_h, block_h, tok_h, gain_h, inv_h, wq_h, wk_h, wv_h,
     q_pack, k_new, v_new, q_long, table,
-    lengths, request, block, tok, gain, inv, wq, wk, wv, x_s, pos_s, t_s, table_s, sems, table_sem,
+    lengths, request, block, tok, gain, inv, wq, wk, wv, x_s, pos_s, table_s, sems, table_sem,
 ):
     third = D // 3
     copies = start_all(
@@ -157,13 +158,12 @@
         q = q + nn_dot(normed[:, i * third : (i + 1) * third], wq[i * third : (i + 1) * third, :])
     for g in range(G):
         roped = rope(q[:, g * HD : (g + 1) * HD])
-        for pair in range(REQ_DEV // 2):
-            q_pack[pair * 32 + g * 8 : pair * 32 + g * 8 + 8, :] = roped[pair * 8 : pair * 8 + 8, :]
-        t_s[g * NEW : (g + 1) * NEW, :] = roped[0:NEW, :]
-    t_s[G * NEW : 16, :] = jnp.zeros((16 - G * NEW, HD), F32)
-    for pair in range(REQ_DEV // 2):
-        q_pack[pair * 32 + 24 : pair * 32 + 32, :] = jnp.zeros((8, HD), F32)
-    packed = t_s[...].astype(BF16)
+        for r in range(REQ_DEV):
+            at = r * LANES + g * NEW
+            q_pack[at : at + NEW, :] = roped[r * NEW : (r + 1) * NEW, :]
+    for r in range(REQ_DEV):
+        q_pack[r * LANES + G * NEW : (r + 1) * LANES, :] = jnp.zeros((LANES - G * NEW, HD), F32)
+    packed = q_pack[0:LANES, :].astype(BF16)
     for i in range(SEQ):
         q_long[i] = packed
     copies[7].wait()
@@ -178,45 +178,43 @@
 
 
 def attend_kernel(
-    table, q_pack, k_new, v_new, q_all, k_c, v_h,
-    att, part0, part,
-    v_c, fresh_s, short_s, top_s, acc_s, sum_s, att_s, o_0, m_0, l_0, long_s, m_s, l_s, o_s, sem,
+    table, q_pack, k_new, v_new, q_all, k_c, v_h, wo_h,
+    att, part0, part, wo,
+    v_c, fresh_s, short_s, top_s, acc_s, sum_s, att_s, long_s, m_s, l_s, o_s, sems,
 ):
-    copy = pltpu.make_async_copy(v_h, v_c, sem)
-    copy.start(priority=1)
-    row = iota((32, ROWS), 0)
-    col = iota((32, ROWS), 1)
-    lane = iota((32, PAGE), 1)
-    half = iota((32, PAGE), 0) % 8 // NEW
+    copies = start_all([(v_h, v_c), (wo_h, wo)], sems)
+    row = iota((LANES, ROWS), 0)
+    col = iota((LANES, ROWS), 1)
+    key_lane = iota((LANES, PAGE), 1)
+
+    def request_score(r):
+        q = q_pack[pl.ds(pl.multiple_of(r * LANES, LANES), LANES), :].astype(BF16)
+        fresh = nt_dot(q, k_new[...]) * SCALE
+        fresh = jnp.where((col // NEW == r) & (col % NEW <= row % NEW), fresh, NEGATIVE)
+        fresh_s[r] = fresh
+        pages = [k_c[table[0, r * SHORT_BLK + i]] for i in range(SHORT_BLK)]
+        s = nt_dot(q, jnp.concatenate(pages, axis=0)) * SCALE
+        used = table[3, 16 + r]
+        tops = []
+        for i in range(SHORT_BLK):
+            part_s = jnp.where(key_lane < used - i * PAGE, s[:, i * PAGE : (i + 1) * PAGE], NEGATIVE)
+            short_s[r, :, i * PAGE : (i + 1) * PAGE] = part_s
+            tops.append(part_s)
+        top = jnp.maximum(jnp.maximum(tops[0], tops[1]), jnp.maximum(tops[2], tops[3]))
+        m = jnp.maximum(jnp.max(top, axis=1, keepdims=True), jnp.max(fresh, axis=1, keepdims=True))
+        top_s[r] = jnp.broadcast_to(m, (LANES, HD))
 
     def pair_score(pair, carry):
-        q = q_pack[pl.ds(pl.multiple_of(pair * 32, 32), 32), :].astype(BF16)
-        fresh = nt_dot(q, k_new[...]) * SCALE
-        fresh_ok = (pair * 2 + row % 8 // NEW == col // NEW) & (col % NEW <= row % NEW)
-        fresh = jnp.where(fresh_ok, fresh, NEGATIVE)
-        fresh_s[pair] = fresh
-        pages = [k_c[table[0, pair * CHUNK + i]] for i in range(CHUNK)]
-        s = nt_dot(q, jnp.concatenate(pages, axis=0)) * SCALE
-        own = jnp.where(half == 0, table[3, 16 + pair * 2], table[3, 17 + pair * 2])
-        tops = []
-        for i in range(CHUNK):
-            inside = (half == i // SHORT_BLK) & (lane < own - i % SHORT_BLK * PAGE)
-            part_s = jnp.where(inside, s[:, i * PAGE : (i + 1) * PAGE], NEGATIVE)
-            short_s[pair, :, i * PAGE : (i + 1) * PAGE] = part_s
-            tops.append(part_s)
-        while len(tops) > 1:
-            tops = [jnp.maximum(x, y) for x, y in zip(tops[::2], tops[1::2])]
-        m = jnp.maximum(jnp.max(tops[0], axis=1, keepdims=True), jnp.max(fresh, axis=1, keepdims=True))
-        top_s[pair] = jnp.broadcast_to(m, (32, HD))
+        request_score(2 * pair)
+        request_score(2 * pair + 1)
         return carry
 
-    lax.fori_loop(0, REQ_DEV // 2, pair_score, 0, unroll=2)
-
-    trips = (table[3, 0] + 1) // 2
+    lax.fori_loop(0, REQ_DEV // 2, pair_score, 0, unroll=4)
+
+    trips = (table[3, 0] + 3) // 4
     m_s[...] = jnp.full((LONGS, 16, HD), NEGATIVE, F32)
     l_s[...] = jnp.zeros((LONGS, 16, HD), F32)
     o_s[...] = jnp.zeros((LONGS, 16, HD), F32)
-    key_lane = iota((16, PAGE), 1)
 
     def entries(chunk):
         words = [table[1 + chunk // (SLOTS // CHUNK), chunk % (SLOTS // CHUNK) * CHUNK + i] for i in range(CHUNK)]
@@ -224,7 +222,7 @@
 
     def long_score(j, carry):
         got = []
-        for chunk in (2 * j, 2 * j + 1):
+        for chunk in (4 * j, 4 * j + 1, 4 * j + 2, 4 * j + 3):
             words, key = entries(chunk)
             pages = [k_c[word & 127] for word in words]
             s = nt_dot(q_all[2 * key], jnp.concatenate(pages, axis=0)) * SCALE
@@ -243,40 +241,40 @@
     lax.fori_loop(0, trips, long_score, 0)
     for k in range(LONGS):
         m_s[k] = jnp.broadcast_to(jnp.maximum(jnp.max(m_s[k], axis=1, keepdims=True), 0.1 * NEGATIVE), (16, HD))
-    copy.wait()
-
-    def pair_sum(pair, carry):
-        m = top_s[pair]
-        w = jnp.exp(fresh_s[pair] - m[:, 0:ROWS]).astype(BF16)
+    copies[0].wait()
+
+    def request_sum(r):
+        m = top_s[r]
+        w = jnp.exp(fresh_s[r] - m[:, 0:ROWS]).astype(BF16)
         total = jnp.sum(w.astype(F32), axis=1, keepdims=True)
         acc = nn_dot(w, v_new[...])
-        ws = [jnp.exp(short_s[pair, :, i * PAGE : (i + 1) * PAGE] - m).astype(BF16) for i in range(CHUNK)]
-        pages = [v_c[table[0, pair * CHUNK + i]] for i in range(CHUNK)]
+        ws = [jnp.exp(short_s[r, :, i * PAGE : (i + 1) * PAGE] - m).astype(BF16) for i in range(SHORT_BLK)]
+        pages = [v_c[table[0, r * SHORT_BLK + i]] for i in range(SHORT_BLK)]
         acc = acc + nn_dot(jnp.concatenate(ws, axis=1), jnp.concatenate(pages, axis=0))
         total = total + jnp.sum(sum(w.astype(F32) for w in ws), axis=1, keepdims=True)
-        acc_s[pair] = acc
-        sum_s[pair] = jnp.broadcast_to(total, (32, HD))
-        out = acc / total
+        acc_s[r] = acc
+        sum_s[r] = jnp.broadcast_to(total, (LANES, HD))
+        return acc / total
+
+    def pair_sum(pair, carry):
+        outs = request_sum(2 * pair), request_sum(2 * pair + 1)
         at = pl.multiple_of(pair * 8, 8)
         for g in range(G):
-            att_s[pl.ds(at, 8), g * HD : (g + 1) * HD] = out[g * 8 : (g + 1) * 8, :]
+            rows = jnp.concatenate([out[g * NEW : (g + 1) * NEW, :] for out in outs], axis=0)
+            att_s[pl.ds(at, 8), g * HD : (g + 1) * HD] = rows
         return carry
 
-    lax.fori_loop(0, REQ_DEV // 2, pair_sum, 0, unroll=2)
+    lax.fori_loop(0, REQ_DEV // 2, pair_sum, 0, unroll=4)
     att[...] = att_s[...]
-    for g in range(G):
-        o_0[g * NEW : (g + 1) * NEW, :] = acc_s[0, g * 8 : g * 8 + NEW, :]
-        m_0[g * NEW : (g + 1) * NEW, :] = top_s[0, g * 8 : g * 8 + NEW, :]
-        l_0[g * NEW : (g + 1) * NEW, :] = sum_s[0, g * 8 : g * 8 + NEW, :]
     eye = (iota((16, HD), 0) == iota((16, HD), 1)) & (iota((16, HD), 0) < G * NEW)
-    part0[...] = o_0[...]
-    part0[12:13, :] = to_row(m_0[...], eye)
-    part0[13:14, :] = to_row(l_0[...], eye)
+    part0[...] = acc_s[0]
+    part0[12:13, :] = to_row(top_s[0], eye)
+    part0[13:14, :] = to_row(sum_s[0], eye)
     part0[14:16, :] = jnp.zeros((2, HD), F32)
 
     def long_sum(j, carry):
         got = []
-        for chunk in (2 * j, 2 * j + 1):
+        for chunk in (4 * j, 4 * j + 1, 4 * j + 2, 4 * j + 3):
             words, key = entries(chunk)
             m = m_s[key]
             ws = [jnp.exp(long_s[chunk, :, i * PAGE : (i + 1) * PAGE] - m).astype(BF16) for i in range(CHUNK)]
@@ -295,6 +293,7 @@
         part[2 * k, 12:14, :] = jnp.concatenate([spread(m_s[k]), spread(total)], axis=0).astype(BF16)
         part[2 * k, 14:16, :] = jnp.zeros((2, HD), BF16)
         part[2 * k + 1] = jnp.zeros((16, HD), BF16)
+    copies[1].wait()
 
 
 def spread(column):
@@ -470,7 +469,7 @@
     q_pack, k_new, v_new, q_long, table = call(
         qkv_kernel,
         (
-            sds((REQ_DEV // 2 * 32, HD), F32),
+            sds((REQ_DEV * LANES, HD), F32),
             sds((ROWS, HD), BF16),
             sds((ROWS, HD), BF16),
             sds((SEQ, 16, HD), BF16),
@@ -489,7 +488,6 @@
             pltpu.VMEM(w_value.shape, BF16),
             pltpu.VMEM((ROWS, D), F32),
             pltpu.VMEM((ROWS, HD), jnp.int32),
-            pltpu.VMEM((16, HD), F32),
             pltpu.VMEM((8, SLOTS), jnp.int32),
             dma((11,)),
             dma(()),
@@ -500,32 +498,34 @@
 
     q_all = lax.all_to_all(q_long, "seq", 0, 0, tiled=True)
 
-    column = pltpu.VMEM((16, HD), F32)
-    longs = pltpu.VMEM((LONGS, 16, HD), F32)
-    pairs = REQ_DEV // 2
-    att, part0, part = call(
+    longs = pltpu.VMEM((LONGS, LANES, HD), F32)
+    each = pltpu.VMEM((REQ_DEV, LANES, HD), F32)
+    att, part0, part, w_out = call(
         attend_kernel,
-        (sds((ROWS, QCOLS), F32), sds((16, HD), F32), sds((SEQ, 16, HD), BF16)),
-        [SMEM] + [VMEM] * 5 + [HBM],
+        (
+            sds((ROWS, QCOLS), F32),
+            sds((LANES, HD), F32),
+            sds((SEQ, LANES, HD), BF16),
+            pltpu.VMEM(w_out.shape, BF16),
+        ),
+        [SMEM] + [VMEM] * 5 + [HBM] * 2,
         [
             pltpu.VMEM(v_cache.shape, BF16),
-            pltpu.VMEM((pairs, 32, ROWS), F32),
-            pltpu.VMEM((pairs, 32, CHUNK * PAGE), F32),
-            pltpu.VMEM((pairs, 32, HD), F32),
-            pltpu.VMEM((pairs, 32, HD), F32),
-            pltpu.VMEM((pairs, 32, HD), F32),
+            pltpu.VMEM((REQ_DEV, LANES, ROWS), F32),
+            pltpu.VMEM((REQ_DEV, LANES, SHORT_BLK * PAGE), F32),
+            each,
+            each,
+            each,
             pltpu.VMEM((ROWS, QCOLS), F32),
-            column,
-            column,
-            column,
-            pltpu.VMEM((2 * SLOTS // CHUNK, 16, CHUNK * PAGE), F32),
+            pltpu.VMEM((2 * SLOTS // CHUNK, LANES, CHUNK * PAGE), F32),
             longs,
             longs,
             longs,
-            dma(()),
+            dma((2,)),
         ],
         10,
-    )(table, q_pack, k_new, v_new, q_all, k_cache, *in_hbm(v_cache))
+    )(table, q_pack, k_new, v_new, q_all, k_cache, *in_hbm(v_cache, w_out))
+    w_out = pltpu.with_memory_space_constraint(w_out, pltpu.VMEM)
 
     parts = lax.all_to_all(part, "seq", 0, 0, tiled=True)
 

time: 68.3 us -> 67.3 us (0.985)
  Pallas kernels: 16.6 us -> 15.7 us
    pallas_call x2, Pallas kernels: 8.95 us -> 8.02 us  [the longest x1 4.46 us: per_device(): call(qkv_kernel, (sds((REQ_DEV * LANES, HD), F32), sds((ROWS, HD), BF16),...]
where the time goes in v2:
time: 67.3 us; the launch traced here: 67.1 us
  blocking collectives  26.6 us (40%)
  waiting for transfers between devices  15.9 us (24%)
  Pallas kernels  15.7 us (23%)
  starting transfers between devices  8.75 us (13%)
    all_to_all x1, blocking collectives, per_device(): q_all = lax.all_to_all(q_long, 'seq', 0, 0, tiled=True)  15.6 us
    ppermute x6, waiting for transfers between devices, along_x(): lax.ppermute(v, 'tensor', [(i, (i + 2 * d) % TEN) for i in range(TEN)])  14.1 us
    all_to_all x1, blocking collectives, per_device(): parts = lax.all_to_all(part, 'seq', 0, 0, tiled=True)  10.9 us
    ppermute x6, starting transfers between devices, along_x(): lax.ppermute(v, 'tensor', [(i, (i + 2 * d) % TEN) for i in range(TEN)])  8 us
    pallas_call x1, Pallas kernels, per_device(): call(qkv_kernel, (sds((REQ_DEV * LANES, HD), F32), sds((ROWS, HD), BF16),...  4.46 us
    pallas_call x1, Pallas kernels, per_device(): call(fetch_kernel, tuple((pltpu.VMEM(w.shape, BF16) for w in weights)), [...  3.78 us
    pallas_call x1, Pallas kernels, per_device(): call(attend_kernel, (sds((ROWS, QCOLS), F32), sds((LANES, HD), F32), sds(...  3.56 us
    ppermute x3, waiting for transfers between devices, swap_core(): return lax.ppermute(v, 'tensor', [(i, i ^ 1) for i in range(TEN)])  1.78 us
  transfers between devices with their start and end apart: 9, of which 7 were waited for; matrix products, arithmetic and copies ran while one was open for 0% of the time, Pallas kernels for 8%

profile of v2, /device:TPU:0, one launch (start us, length us, event | category | flops | bytes accessed | tf_op | source)
XLA Modules:
  0.0 67.1 jit_solution(2001032929776073260)
XLA Ops:
  0.0 0.0 copy-start
  0.0 4.5 %shard_map.154 = (f32[256,128]{1,0:T(8,128)S(1)}, bf16[64,128]{1,0:T(8,128)(2,1)S(1)}, bf16[64,128]{1,0:T(8,128)(2,1)S(1)}, bf16[16,16,128]{2,1,0:T(8,128)(2,1)S(1)}, s32[8,128]{1,0:T(8,128)S(4)}) custom-call(s32[256]{0:T(256)} %lengths_h.1, s32[128]{0:T(128)} %request_h.1, s32[128]{0:T(128)} %block_h.1, bf16[16,4,3072]{2,1,0:T(4,128)(2,1)} %tok.1, ...), custom_call_target="tpu_custom_call" | custom-call | tf_op jit(solution)/shard_map/pallas_call | solution.py:469
  4.5 15.6 %all_to_all.10.q_all = bf16[16,16,128]{2,1,0:T(8,128)(2,1)S(1)} all-to-all(bf16[16,16,128]{2,1,0:T(8,128)(2,1)S(1)} %get-tuple-element.32), channel_id=1, replica_groups=mesh['seq'=16,'tensor'=8] {'seq'}, dimensions={0} | all-to-all | bytes 131072 | tf_op jit(solution)/shard_map/all_to_all | solution.py:499
  20.1 0.0 copy-done
  20.1 3.6 %shard_map.155 = (f32[64,384]{1,0:T(8,128)S(1)}, f32[16,128]{1,0:T(8,128)S(1)}, bf16[16,16,128]{2,1,0:T(8,128)(2,1)S(1)}, bf16[384,3072]{1,0:T(8,128)(2,1)S(1)}) custom-call(s32[8,128]{1,0:T(8,128)S(4)} %get-tuple-element.28.table, f32[256,128]{1,0:T(8,128)S(1)} %get-tuple-element.29.q_pack, bf16[64,128]{1,0:T(8,128)(2,1)S(1)} %get-tuple-element.30.k_new, ...), custom_call_target="tpu_custom_call" | custom-call | tf_op jit(solution)/shard_map/pallas_call | solution.py:503
  23.7 0.0 copy-start.1
  23.7 10.9 %all_to_all.11.parts = bf16[16,16,128]{2,1,0:T(8,128)(2,1)S(1)} all-to-all(bf16[16,16,128]{2,1,0:T(8,128)(2,1)S(1)} %get-tuple-element.35), channel_id=1, replica_groups=mesh['seq'=16,'tensor'=8] {'seq'}, dimensions={0} | all-to-all | bytes 131072 | tf_op jit(solution)/shard_map/all_to_all | solution.py:530
  34.6 0.6 shard_map.156
  35.2 0.1 collective-permute-start
  35.3 0.3 shard_map.157.keep
  35.6 1.1 %collective-permute-done.got = bf16[4,64,384]{2,1,0:T(8,128)(2,1)S(1)} collective-permute-done((bf16[4,64,384]{2,1,0:T(8,128)(2,1)S(1)}, bf16[4,64,384]{2,1,0:T(8,128)(2,1)S(1)}, u32[]{:S(2)}, u32[]{:S(2)}) %collective-permute-start) | collective-permute-done | bytes 196640 | tf_op jit(solution)/shard_map/ppermute | solution.py:429
  36.7 0.1 shard_map.158.own.after
  36.8 2.8 %collective-permute-start.3 = (bf16[4,64,384]{2,1,0:T(8,128)(2,1)S(1)}, bf16[4,64,384]{2,1,0:T(8,128)(2,1)S(1)}, u32[]{:S(2)}, u32[]{:S(2)}) collective-permute-start(bf16[4,64,384]{2,1,0:T(8,128)(2,1)S(1)} %shard_map.158.own.after), channel_id=1, source_target_pairs={{0,6},{1,7},{2,0},{3,1},{4,2},{5,3},{6,4},{7,5},{8,14},{9,15},{10,... | collective-permute-start | bytes 589832 | tf_op jit(solution)/shard_map/ppermute | solution.py:433
  39.6 0.8 %collective-permute-start.2 = (bf16[4,64,384]{2,1,0:T(8,128)(2,1)S(1)}, bf16[4,64,384]{2,1,0:T(8,128)(2,1)S(1)}, u32[]{:S(2)}, u32[]{:S(2)}) collective-permute-start(bf16[4,64,384]{2,1,0:T(8,128)(2,1)S(1)} %shard_map.158.own.after), channel_id=1, source_target_pairs={{0,4},{1,5},{2,6},{3,7},{4,0},{5,1},{6,2},{7,3},{8,12},{9,13},{10,... | collective-permute-start | bytes 589832 | tf_op jit(solution)/shard_map/ppermute | solution.py:433
  40.4 0.9 %collective-permute-start.1 = (bf16[4,64,384]{2,1,0:T(8,128)(2,1)S(1)}, bf16[4,64,384]{2,1,0:T(8,128)(2,1)S(1)}, u32[]{:S(2)}, u32[]{:S(2)}) collective-permute-start(bf16[4,64,384]{2,1,0:T(8,128)(2,1)S(1)} %shard_map.158.own.after), channel_id=1, source_target_pairs={{0,2},{1,3},{2,4},{3,5},{4,6},{5,7},{6,0},{7,1},{8,10},{9,11},{10,... | collective-permute-start | bytes 589832 | tf_op jit(solution)/shard_map/ppermute | solution.py:433
  41.3 7.0 %collective-permute-done.3.r3 = bf16[4,64,384]{2,1,0:T(8,128)(2,1)S(1)} collective-permute-done((bf16[4,64,384]{2,1,0:T(8,128)(2,1)S(1)}, bf16[4,64,384]{2,1,0:T(8,128)(2,1)S(1)}, u32[]{:S(2)}, u32[]{:S(2)}) %collective-permute-start.3) | collective-permute-done | bytes 196640 | tf_op jit(solution)/shard_map/ppermute | solution.py:433
  48.3 0.6 collective-permute-done.2.r2
  48.9 3.1 %collective-permute-done.1.r1 = bf16[4,64,384]{2,1,0:T(8,128)(2,1)S(1)} collective-permute-done((bf16[4,64,384]{2,1,0:T(8,128)(2,1)S(1)}, bf16[4,64,384]{2,1,0:T(8,128)(2,1)S(1)}, u32[]{:S(2)}, u32[]{:S(2)}) %collective-permute-start.1) | collective-permute-done | bytes 196640 | tf_op jit(solution)/shard_map/ppermute | solution.py:433
  52.0 0.0 copy-done.1
  52.0 0.2 shard_map.159.mine.res
  52.1 0.0 copy-start.2
  52.1 0.1 collective-permute-start.4
  52.2 3.8 %shard_map.160 = (bf16[3072,512]{1,0:T(8,128)(2,1)S(1)}, bf16[3072,512]{1,0:T(8,128)(2,1)S(1)}, bf16[512,3072]{1,0:T(8,128)(2,1)S(1)}) custom-call(bf16[4,64,384]{2,1,0:T(8,128)(2,1)S(1)} %shard_map.158.own.after, bf16[3072,512]{1,0:T(8,128)(2,1)} %wg_h.1, bf16[3072,512]{1,0:T(8,128)(2,1)} %wu_h.1, bf16[512,3072]{1,0:T(8,128)(2,1)} %wd_h.1), custom_call_target="tpu_custom_call" | custom-call | tf_op jit(solution)/shard_map/pallas_call | solution.py:544
  56.0 0.0 copy-done.2
  56.0 0.7 %shard_map.161 = (f32[64,512]{1,0:T(8,128)S(1)}, f32[64,512]{1,0:T(8,128)S(1)}, f32[64,128]{1,0:T(8,128)S(1)}) custom-call(bf16[4,64,384]{2,1,0:T(8,128)(2,1)S(1)} %shard_map.159.mine.res, bf16[3072]{0:T(1024)(128)(2,1)S(1)} %copy-done.2, bf16[3072,512]{1,0:T(8,128)(2,1)S(1)} %get-tuple-element.39.w_gate, bf16[3072,512]{1,0:T(8,128)(2,1)S(1)} %get-tuple-element.40.w_up), custom_call_target="tpu_custom_call" | custom-call | tf_op jit(solution)/shard_map/pallas_call | solution.py:555
  56.7 0.0 collective-permute-done.4.other
  56.7 1.0 %shard_map.162 = (bf16[64,512]{1,0:T(8,128)(2,1)S(1)}, bf16[4,64,384]{2,1,0:T(8,128)(2,1)S(1)}) custom-call(bf16[4,64,384]{2,1,0:T(8,128)(2,1)S(1)} %collective-permute-done.4.other, bf16[3072]{0:T(1024)(128)(2,1)S(1)} %copy-done.2, f32[64,512]{1,0:T(8,128)S(1)} %get-tuple-element.41.gate, f32[64,512]{1,0:T(8,128)S(1)} %get-tuple-element.42.up, ...), custom_call_target="tpu_custom_call" | custom-call | tf_op jit(solution)/shard_map/pallas_call | solution.py:558
  57.8 0.6 collective-permute-start.5
  58.4 0.4 shard_map.163.keep
  58.7 0.7 %collective-permute-done.5.got = bf16[4,64,384]{2,1,0:T(8,128)(2,1)S(1)} collective-permute-done((bf16[4,64,384]{2,1,0:T(8,128)(2,1)S(1)}, bf16[4,64,384]{2,1,0:T(8,128)(2,1)S(1)}, u32[]{:S(2)}, u32[]{:S(2)}) %collective-permute-start.5) | collective-permute-done | bytes 196640 | tf_op jit(solution)/shard_map/ppermute | solution.py:429
  59.5 0.1 collective-permute-start.6
  59.6 2.1 %collective-permute-start.7 = (bf16[64,384]{1,0:T(8,128)(2,1)S(1)}, bf16[64,384]{1,0:T(8,128)(2,1)S(1)}, u32[]{:S(2)}, u32[]{:S(2)}) collective-permute-start(bf16[64,384]{1,0:T(8,128)(2,1)S(1)} %get-tuple-element.49), channel_id=1, source_target_pairs={{0,4},{1,5},{2,6},{3,7},{4,0},{5,1},{6,2},{7,3},{8,12},{9,13},{10,... | collective-permute-start | bytes 147464 | tf_op jit(solution)/shard_map/ppermute | solution.py:433
  61.6 1.4 %collective-permute-start.8 = (bf16[64,384]{1,0:T(8,128)(2,1)S(1)}, bf16[64,384]{1,0:T(8,128)(2,1)S(1)}, u32[]{:S(2)}, u32[]{:S(2)}) collective-permute-start(bf16[64,384]{1,0:T(8,128)(2,1)S(1)} %get-tuple-element.50), channel_id=1, source_target_pairs={{0,6},{1,7},{2,0},{3,1},{4,2},{5,3},{6,4},{7,5},{8,14},{9,15},{10,... | collective-permute-start | bytes 147464 | tf_op jit(solution)/shard_map/ppermute | solution.py:433
  63.0 2.8 %collective-permute-done.6.r1 = bf16[64,384]{1,0:T(8,128)(2,1)S(1)} collective-permute-done((bf16[64,384]{1,0:T(8,128)(2,1)S(1)}, bf16[64,384]{1,0:T(8,128)(2,1)S(1)}, u32[]{:S(2)}, u32[]{:S(2)}) %collective-permute-start.6) | collective-permute-done | bytes 49184 | tf_op jit(solution)/shard_map/ppermute | solution.py:433
  65.8 0.0 collective-permute-done.7.r2
  65.8 0.6 collective-permute-done.8.r3
  66.4 0.7 shard_map.165
  (1 shorter events, 0.0 us)
Async XLA Ops:
  0.0 20.1 %copy-start = (bf16[128,1,128,128]{3,2,1,0:T(8,128)(2,1)S(1)}, bf16[128,1,128,128]{3,2,1,0:T(8,128)(2,1)}, u32[]{:S(2)}) copy-start(bf16[128,1,128,128]{3,2,1,0:T(8,128)(2,1)} %param.20) | copy-start | bytes 12582916
  23.7 28.3 %copy-start.1 = (bf16[16,4,3072]{2,1,0:T(4,128)(2,1)S(1)}, bf16[16,4,3072]{2,1,0:T(4,128)(2,1)}, u32[]{:S(2)}) copy-start(bf16[16,4,3072]{2,1,0:T(4,128)(2,1)} %tok.1) | copy-start | bytes 1179652
  35.2 1.5 %collective-permute-start = (bf16[4,64,384]{2,1,0:T(8,128)(2,1)S(1)}, bf16[4,64,384]{2,1,0:T(8,128)(2,1)S(1)}, u32[]{:S(2)}, u32[]{:S(2)}) collective-permute-start(bf16[4,64,384]{2,1,0:T(8,128)(2,1)S(1)} %get-tuple-element.38), channel_id=1, source_target_pairs={{0,1},{1,0},{2,3},{3,2},{4,5},{5,4},{6,7},{7,6},{8,9},{9,8},{10,11... | collective-permute-start | bytes 589832 | tf_op jit(solution)/shard_map/ppermute | solution.py:429
  36.8 11.5 %collective-permute-start.3 = (bf16[4,64,384]{2,1,0:T(8,128)(2,1)S(1)}, bf16[4,64,384]{2,1,0:T(8,128)(2,1)S(1)}, u32[]{:S(2)}, u32[]{:S(2)}) collective-permute-start(bf16[4,64,384]{2,1,0:T(8,128)(2,1)S(1)} %shard_map.158.own.after), channel_id=1, source_target_pairs={{0,6},{1,7},{2,0},{3,1},{4,2},{5,3},{6,4},{7,5},{8,14},{9,15},{10,... | collective-permute-start | bytes 589832 | tf_op jit(solution)/shard_map/ppermute | solution.py:433
  39.6 9.3 %collective-permute-start.2 = (bf16[4,64,384]{2,1,0:T(8,128)(2,1)S(1)}, bf16[4,64,384]{2,1,0:T(8,128)(2,1)S(1)}, u32[]{:S(2)}, u32[]{:S(2)}) collective-permute-start(bf16[4,64,384]{2,1,0:T(8,128)(2,1)S(1)} %shard_map.158.own.after), channel_id=1, source_target_pairs={{0,4},{1,5},{2,6},{3,7},{4,0},{5,1},{6,2},{7,3},{8,12},{9,13},{10,... | collective-permute-start | bytes 589832 | tf_op jit(solution)/shard_map/ppermute | solution.py:433
  40.4 11.6 %collective-permute-start.1 = (bf16[4,64,384]{2,1,0:T(8,128)(2,1)S(1)}, bf16[4,64,384]{2,1,0:T(8,128)(2,1)S(1)}, u32[]{:S(2)}, u32[]{:S(2)}) collective-permute-start(bf16[4,64,384]{2,1,0:T(8,128)(2,1)S(1)} %shard_map.158.own.after), channel_id=1, source_target_pairs={{0,2},{1,3},{2,4},{3,5},{4,6},{5,7},{6,0},{7,1},{8,10},{9,11},{10,... | collective-permute-start | bytes 589832 | tf_op jit(solution)/shard_map/ppermute | solution.py:433
  52.1 3.9 %copy-start.2 = (bf16[3072]{0:T(1024)(128)(2,1)S(1)}, bf16[3072]{0:T(1024)(128)(2,1)}, u32[]{:S(2)}) copy-start(bf16[3072]{0:T(1024)(128)(2,1)} %gain.3) | copy-start | bytes 18436
  52.1 4.6 %collective-permute-start.4 = (bf16[4,64,384]{2,1,0:T(8,128)(2,1)S(1)}, bf16[4,64,384]{2,1,0:T(8,128)(2,1)S(1)}, u32[]{:S(2)}, u32[]{:S(2)}) collective-permute-start(bf16[4,64,384]{2,1,0:T(8,128)(2,1)S(1)} %shard_map.159.mine.res), channel_id=1, source_target_pairs={{0,1},{1,0},{2,3},{3,2},{4,5},{5,4},{6,7},{7,6},{8,9},{9,8},{10,11... | collective-permute-start | bytes 589832 | tf_op jit(solution)/shard_map/ppermute | solution.py:429
  57.8 1.6 %collective-permute-start.5 = (bf16[4,64,384]{2,1,0:T(8,128)(2,1)S(1)}, bf16[4,64,384]{2,1,0:T(8,128)(2,1)S(1)}, u32[]{:S(2)}, u32[]{:S(2)}) collective-permute-start(bf16[4,64,384]{2,1,0:T(8,128)(2,1)S(1)} %get-tuple-element.46), channel_id=1, source_target_pairs={{0,1},{1,0},{2,3},{3,2},{4,5},{5,4},{6,7},{7,6},{8,9},{9,8},{10,11... | collective-permute-start | bytes 589832 | tf_op jit(solution)/shard_map/ppermute | solution.py:429
  59.5 6.4 %collective-permute-start.6 = (bf16[64,384]{1,0:T(8,128)(2,1)S(1)}, bf16[64,384]{1,0:T(8,128)(2,1)S(1)}, u32[]{:S(2)}, u32[]{:S(2)}) collective-permute-start(bf16[64,384]{1,0:T(8,128)(2,1)S(1)} %get-tuple-element.48), channel_id=1, source_target_pairs={{0,2},{1,3},{2,4},{3,5},{4,6},{5,7},{6,0},{7,1},{8,10},{9,11},{10,... | collective-permute-start | bytes 147464 | tf_op jit(solution)/shard_map/ppermute | solution.py:433
  59.6 6.3 %collective-permute-start.7 = (bf16[64,384]{1,0:T(8,128)(2,1)S(1)}, bf16[64,384]{1,0:T(8,128)(2,1)S(1)}, u32[]{:S(2)}, u32[]{:S(2)}) collective-permute-start(bf16[64,384]{1,0:T(8,128)(2,1)S(1)} %get-tuple-element.49), channel_id=1, source_target_pairs={{0,4},{1,5},{2,6},{3,7},{4,0},{5,1},{6,2},{7,3},{8,12},{9,13},{10,... | collective-permute-start | bytes 147464 | tf_op jit(solution)/shard_map/ppermute | solution.py:433
  61.6 4.8 %collective-permute-start.8 = (bf16[64,384]{1,0:T(8,128)(2,1)S(1)}, bf16[64,384]{1,0:T(8,128)(2,1)S(1)}, u32[]{:S(2)}, u32[]{:S(2)}) collective-permute-start(bf16[64,384]{1,0:T(8,128)(2,1)S(1)} %get-tuple-element.50), channel_id=1, source_target_pairs={{0,6},{1,7},{2,0},{3,1},{4,2},{5,3},{6,4},{7,5},{8,14},{9,15},{10,... | collective-permute-start | bytes 147464 | tf_op jit(solution)/shard_map/ppermute | solution.py:433
